TPU v7x, 32 devices: a whole 2x2x4 slice. The times are simulated.
32 devices in a mesh: dp: 16 (over z, x, core), tensor: 2 (over y).
Axes of the slice: x: 2, y: 2, z: 4, core: 2. Of those that a mesh axis runs over, the one named last changes fastest.
Arguments:
- x_given: bfloat16 [16, 1024, 768], P(None, ('dp', 'tensor')), may hold values from -6 to 6
- dealing: int32 [16], replicated, may hold values from 0 to 15, each once
- seq_lengths: int32 [16], replicated, may hold values from 256 to 1024, as said below
- first_gain: bfloat16 [768], P('dp'), may hold values from 0.099609375 to 1.8984375
- query_weight: bfloat16 [768, 768], P('dp', 'tensor'), may hold values from -0.3125 to 0.3125
- key_weight: bfloat16 [768, 768], P('dp', 'tensor'), may hold values from -0.3125 to 0.3125
- value_weight: bfloat16 [768, 768], P('dp', 'tensor'), may hold values from -0.21875 to 0.21875
- output_weight: bfloat16 [768, 768], P('dp', 'tensor'), may hold values from -0.875 to 0.875
- second_gain: bfloat16 [768], P('dp'), may hold values from 0.099609375 to 1.8984375
- gate_weight: bfloat16 [768, 2560], P('dp', 'tensor'), may hold values from -0.21875 to 0.21875
- up_weight: bfloat16 [768, 2560], P('dp', 'tensor'), may hold values from -0.21875 to 0.21875
- down_weight: bfloat16 [768, 2560], P('dp', 'tensor'), may hold values from -0.25 to 0.25
- grad_output: bfloat16 [16, 16, 2, 32, 768], P('dp', None, 'tensor'), may hold values from -6 to 6
Outputs:
- layer_out: bfloat16 [16, 16, 2, 32, 768], P('dp', None, 'tensor')
- grad_in: bfloat16 [16, 1024, 768], P(None, ('dp', 'tensor'))
- grad_first_gain: float32 [768], P('dp')
- grad_query_weight: float32 [768, 768], P('dp', 'tensor')
- grad_key_weight: float32 [768, 768], P('dp', 'tensor')
- grad_value_weight: float32 [768, 768], P('dp', 'tensor')
- grad_output_weight: float32 [768, 768], P('dp', 'tensor')
- grad_second_gain: float32 [768], P('dp')
- grad_gate_weight: float32 [768, 2560], P('dp', 'tensor')
- grad_up_weight: float32 [768, 2560], P('dp', 'tensor')
- grad_down_weight: float32 [768, 2560], P('dp', 'tensor')
Inputs may be any that keep to these rules, and one draw needn't show every extreme that they name: `dealing`: a permutation of the 16 sequences. `seq_lengths`: some sequence is live at all 1024 positions.
All inputs are finite; a program needn't handle non-finite values.
Results may differ from a plain program's by a relative error of at most 0.025.
Values may be sent and summed in bfloat16 or wider, within the bound.
A program may use at most 128 MiB of HBM per device.

v0:
```python
import jax
import jax.numpy as jnp
from jax import lax
from jax.sharding import PartitionSpec as P

HD = 48


EPS = 1e-05
BASE = 10000.0


def tables(positions, head_size):
    freq_index = jnp.arange(head_size // 2, dtype=jnp.float32)
    frequency = BASE ** (-2.0 * freq_index / head_size)
    angles = positions[:, None] * frequency[None, :]
    return (jnp.cos(angles)[:, None, :], jnp.sin(angles)[:, None, :])


def rotary(values, cosine, sine_table):
    half_width = values.shape[-1] // 2
    first_half = values[..., :half_width]
    second_half = values[..., half_width:]
    return jnp.concatenate(
        [
            first_half * cosine - second_half * sine_table,
            second_half * cosine + first_half * sine_table,
        ],
        axis=-1,
    )


def rotary_back(values, cosine, sine_table):
    half_width = values.shape[-1] // 2
    first_half = values[..., :half_width]
    second_half = values[..., half_width:]
    return jnp.concatenate(
        [
            first_half * cosine + second_half * sine_table,
            second_half * cosine - first_half * sine_table,
        ],
        axis=-1,
    )


def row_dot(left_side, right_side):
    return jnp.dot(left_side, right_side, preferred_element_type=jnp.float32)


def dot_trans(left_side, right_side):
    return lax.dot_general(
        left_side, right_side, (((1,), (1,)), ((), ())), preferred_element_type=jnp.float32
    )


def dot_first(left_side, right_side):
    return lax.dot_general(
        left_side, right_side, (((0,), (0,)), ((), ())), preferred_element_type=jnp.float32
    )


def tensor_major(values, groups, pieces, piece_rows):
    columns = values.shape[1]
    return (
        values.reshape(groups, pieces, piece_rows, columns)
        .transpose(1, 0, 2, 3)
        .reshape(groups * pieces * piece_rows, columns)
    )


def rms_back(grad_normed, x_rows, scale_rows, gain):
    normed = x_rows * scale_rows
    weighted = grad_normed * gain
    x_grad = scale_rows * (weighted - normed * jnp.mean(weighted * normed, axis=-1, keepdims=True))
    return (x_grad, jnp.sum(grad_normed * normed, axis=0))


def block_scores(queries, key_rows, query_start, key_start, block_rows, score_scale):
    query_part = lax.dynamic_slice_in_dim(queries, query_start, block_rows, 0)
    key_part = lax.dynamic_slice_in_dim(key_rows, key_start, block_rows, 0)
    scores = (
        jnp.einsum("qhd,khd->hqk", query_part, key_part, preferred_element_type=jnp.float32)
        * score_scale
    )
    row_offsets = jnp.arange(block_rows)
    allowed = (key_start + row_offsets)[None, :] <= (query_start + row_offsets)[:, None]
    return jnp.where(allowed[None], scores, -1e30)


def attend_forward(queries, key_rows, value_rows, live_blocks, block_rows, score_scale):
    seq_len, heads, head_size = queries.shape

    def one_block(query_index, state_now):
        outputs, log_sums = state_now
        query_start = query_index * block_rows

        def stats(key_index, carried):
            running, exp_total = carried
            scores = block_scores(
                queries, key_rows, query_start, key_index * block_rows, block_rows, score_scale
            )
            newest = jnp.maximum(running, jnp.max(scores, axis=-1))
            exp_total = exp_total * jnp.exp(running - newest) + jnp.sum(
                jnp.exp(scores - newest[..., None]), axis=-1
            )
            return (newest, exp_total)

        initial = (
            jnp.full((heads, block_rows), -1e30, jnp.float32),
            jnp.zeros((heads, block_rows), jnp.float32),
        )
        running, exp_total = lax.fori_loop(0, query_index + 1, stats, initial)
        log_sum = running + jnp.log(exp_total)

        def accumulate(key_index, accumulated):
            key_start = key_index * block_rows
            scores = block_scores(
                queries, key_rows, query_start, key_start, block_rows, score_scale
            )
            prob_low = jnp.exp(scores - log_sum[..., None]).astype(jnp.bfloat16)
            value_part = lax.dynamic_slice_in_dim(value_rows, key_start, block_rows, 0)
            return accumulated + jnp.einsum(
                "hqk,khd->qhd", prob_low, value_part, preferred_element_type=jnp.float32
            )

        result = lax.fori_loop(
            0, query_index + 1, accumulate, jnp.zeros((block_rows, heads, head_size), jnp.float32)
        )
        outputs = lax.dynamic_update_slice_in_dim(outputs, result, query_start, 0)
        log_sums = lax.dynamic_update_slice_in_dim(log_sums, log_sum, query_start, 1)
        return (outputs, log_sums)

    initial = (
        jnp.zeros((seq_len, heads, head_size), jnp.float32),
        jnp.zeros((heads, seq_len), jnp.float32),
    )
    return lax.fori_loop(0, live_blocks, one_block, initial)


def attend_backward(
    queries, key_rows, value_rows, outputs, log_sums, out_grad, live_blocks, block_rows, score_scale
):
    seq_len, heads, head_size = queries.shape
    row_delta = jnp.einsum("qhd,qhd->hq", out_grad.astype(jnp.float32), outputs)

    def one_block(query_index, state_now):
        query_grads, key_grads, value_grads = state_now
        query_start = query_index * block_rows
        query_part = lax.dynamic_slice_in_dim(queries, query_start, block_rows, 0)
        grad_part = lax.dynamic_slice_in_dim(out_grad, query_start, block_rows, 0)
        logsum_part = lax.dynamic_slice_in_dim(log_sums, query_start, block_rows, 1)
        delta_part = lax.dynamic_slice_in_dim(row_delta, query_start, block_rows, 1)

        def inner(key_index, carried):
            query_acc, key_grads, value_grads = carried
            key_start = key_index * block_rows
            key_part = lax.dynamic_slice_in_dim(key_rows, key_start, block_rows, 0)
            value_part = lax.dynamic_slice_in_dim(value_rows, key_start, block_rows, 0)
            scores = block_scores(
                queries, key_rows, query_start, key_start, block_rows, score_scale
            )
            prob_soft = jnp.exp(scores - logsum_part[..., None])
            prob_low = prob_soft.astype(jnp.bfloat16)
            prob_grad = jnp.einsum(
                "qhd,khd->hqk", grad_part, value_part, preferred_element_type=jnp.float32
            )
            score_grad = (prob_soft * (prob_grad - delta_part[..., None])).astype(jnp.bfloat16)
            query_acc = (
                query_acc
                + jnp.einsum(
                    "hqk,khd->qhd", score_grad, key_part, preferred_element_type=jnp.float32
                )
                * score_scale
            )
            key_new = (
                jnp.einsum(
                    "hqk,qhd->khd", score_grad, query_part, preferred_element_type=jnp.float32
                )
                * score_scale
            )
            value_new = jnp.einsum(
                "hqk,qhd->khd", prob_low, grad_part, preferred_element_type=jnp.float32
            )
            key_old = lax.dynamic_slice_in_dim(key_grads, key_start, block_rows, 0)
            value_old = lax.dynamic_slice_in_dim(value_grads, key_start, block_rows, 0)
            key_grads = lax.dynamic_update_slice_in_dim(key_grads, key_old + key_new, key_start, 0)
            value_grads = lax.dynamic_update_slice_in_dim(
                value_grads, value_old + value_new, key_start, 0
            )
            return (query_acc, key_grads, value_grads)

        initial = (jnp.zeros((block_rows, heads, head_size), jnp.float32), key_grads, value_grads)
        query_acc, key_grads, value_grads = lax.fori_loop(0, query_index + 1, inner, initial)
        query_grads = lax.dynamic_update_slice_in_dim(query_grads, query_acc, query_start, 0)
        return (query_grads, key_grads, value_grads)

    zero_grads = jnp.zeros((seq_len, heads, head_size), jnp.float32)
    return lax.fori_loop(0, live_blocks, one_block, (zero_grads, zero_grads, zero_grads))


def body(
    x_given,
    dealing,
    seq_lengths,
    first_gain,
    query_weight,
    key_weight,
    value_weight,
    output_weight,
    second_gain,
    gate_weight,
    up_weight,
    down_weight,
    grad_output,
):
    groups = lax.axis_size("dp")
    pieces = lax.axis_size("tensor")
    group_index = lax.axis_index("dp")
    piece_index = lax.axis_index("tensor")
    seq_count, piece_rows, features = x_given.shape
    tokens = groups * piece_rows
    seq_len = tokens * pieces
    head_width = query_weight.shape[1]
    heads_local = head_width // HD
    block_rows = min(512, seq_len)
    score_scale = HD ** (-0.5)
    sequence = dealing[group_index]
    length = seq_lengths[sequence]
    live_blocks = (length + block_rows - 1) // block_rows
    outgoing = jnp.take(x_given, dealing, axis=0)
    arrived = lax.all_to_all(outgoing, "dp", split_axis=0, concat_axis=1, tiled=True)
    x_rows = arrived.reshape(tokens, features).astype(jnp.float32)
    row_ids = jnp.arange(tokens)
    positions_local = (
        row_ids // piece_rows * pieces + piece_index
    ) * piece_rows + row_ids % piece_rows
    live_rows = (positions_local < length).astype(jnp.float32)[:, None]
    columns = (
        lax.all_gather(gate_weight, "tensor", axis=1, tiled=True),
        lax.all_gather(up_weight, "tensor", axis=1, tiled=True),
        lax.all_gather(down_weight, "tensor", axis=1, tiled=True),
    )
    gathered = (
        lax.all_gather(first_gain, "dp", axis=0, tiled=True),
        lax.all_gather(second_gain, "dp", axis=0, tiled=True),
        lax.all_gather(query_weight, "dp", axis=0, tiled=True),
        lax.all_gather(key_weight, "dp", axis=0, tiled=True),
        lax.all_gather(value_weight, "dp", axis=0, tiled=True),
        lax.all_gather(output_weight, "dp", axis=0, tiled=True),
        lax.all_gather(columns[0], "dp", axis=0, tiled=True),
        lax.all_gather(columns[1], "dp", axis=0, tiled=True),
        lax.all_gather(columns[2], "dp", axis=0, tiled=True),
    )
    (
        gain_one,
        gain_two,
        query_full,
        key_full,
        value_full,
        out_full,
        gate_full,
        up_full,
        down_full,
    ) = gathered
    qkv_weight = jnp.concatenate([query_full, key_full, value_full], axis=1)
    scale_one = lax.rsqrt(jnp.mean(x_rows * x_rows, axis=-1, keepdims=True) + EPS)
    normed = (x_rows * scale_one * gain_one).astype(jnp.bfloat16)
    normed_full = lax.all_gather(
        normed.reshape(groups, 1, piece_rows, features), "tensor", axis=1, tiled=True
    ).reshape(seq_len, features)
    projected = row_dot(normed_full, qkv_weight)
    cosine, sine_table = tables(jnp.arange(seq_len, dtype=jnp.float32), HD)
    queries = rotary(
        projected[:, :head_width].reshape(seq_len, heads_local, HD), cosine, sine_table
    ).astype(jnp.bfloat16)
    key_rows = rotary(
        projected[:, head_width : 2 * head_width].reshape(seq_len, heads_local, HD),
        cosine,
        sine_table,
    ).astype(jnp.bfloat16)
    value_rows = (
        projected[:, 2 * head_width :].astype(jnp.bfloat16).reshape(seq_len, heads_local, HD)
    )
    mixed, log_sums = attend_forward(
        queries, key_rows, value_rows, live_blocks, block_rows, score_scale
    )
    mixed_low = mixed.reshape(seq_len, head_width).astype(jnp.bfloat16)
    mixed_major = tensor_major(mixed_low, groups, pieces, piece_rows)
    attention = lax.psum_scatter(
        dot_trans(mixed_major, out_full).astype(jnp.bfloat16),
        "tensor",
        scatter_dimension=0,
        tiled=True,
    ).astype(jnp.float32)
    hidden_one = x_rows + live_rows * attention
    scale_two = lax.rsqrt(jnp.mean(hidden_one * hidden_one, axis=-1, keepdims=True) + EPS)
    normed_two = (hidden_one * scale_two * gain_two).astype(jnp.bfloat16)
    gate_act = row_dot(normed_two, gate_full)
    up_act = row_dot(normed_two, up_full)
    sigmoid_act = jax.nn.sigmoid(gate_act)
    silu_act = gate_act * sigmoid_act
    hidden = (silu_act * up_act).astype(jnp.bfloat16)
    branch = dot_trans(hidden, down_full)
    result = hidden_one + live_rows * branch
    layer_out = result.astype(jnp.bfloat16).reshape(1, groups, 1, piece_rows, features)
    out_grad = grad_output.reshape(tokens, features).astype(jnp.float32)
    branch_grad = (live_rows * out_grad).astype(jnp.bfloat16)
    hidden_grad = row_dot(branch_grad, down_full)
    down_term = dot_first(branch_grad, hidden)
    gate_grad = (
        hidden_grad * up_act * sigmoid_act * (1.0 + gate_act * (1.0 - sigmoid_act))
    ).astype(jnp.bfloat16)
    up_grad = (hidden_grad * silu_act).astype(jnp.bfloat16)
    normed_two_grad = dot_trans(gate_grad, gate_full) + dot_trans(up_grad, up_full)
    gate_term = dot_first(normed_two, gate_grad)
    up_term = dot_first(normed_two, up_grad)
    hidden_one_grad, gain_two_term = rms_back(normed_two_grad, hidden_one, scale_two, gain_two)
    hidden_one_grad = hidden_one_grad + out_grad
    attention_grad = (live_rows * hidden_one_grad).astype(jnp.bfloat16)
    attention_full = lax.all_gather(
        attention_grad.reshape(groups, 1, piece_rows, features), "tensor", axis=1, tiled=True
    ).reshape(seq_len, features)
    mixed_grad = row_dot(attention_full, out_full).astype(jnp.bfloat16)
    out_term = dot_first(attention_full, mixed_low)
    query_grads, key_grads, value_grads = attend_backward(
        queries,
        key_rows,
        value_rows,
        mixed,
        log_sums,
        mixed_grad.reshape(seq_len, heads_local, HD),
        live_blocks,
        block_rows,
        score_scale,
    )
    query_back = (
        rotary_back(query_grads, cosine, sine_table)
        .reshape(seq_len, head_width)
        .astype(jnp.bfloat16)
    )
    key_back = (
        rotary_back(key_grads, cosine, sine_table).reshape(seq_len, head_width).astype(jnp.bfloat16)
    )
    value_back = value_grads.reshape(seq_len, head_width).astype(jnp.bfloat16)
    projected_grad = jnp.concatenate([query_back, key_back, value_back], axis=1)
    qkv_term = dot_first(normed_full, projected_grad)
    grad_major = tensor_major(projected_grad, groups, pieces, piece_rows)
    normed_grad = lax.psum_scatter(
        dot_trans(grad_major, qkv_weight).astype(jnp.bfloat16),
        "tensor",
        scatter_dimension=0,
        tiled=True,
    ).astype(jnp.float32)
    input_grad, gain_one_term = rms_back(normed_grad, x_rows, scale_one, gain_one)
    input_grad = input_grad + hidden_one_grad
    returned = lax.all_to_all(
        input_grad.astype(jnp.bfloat16).reshape(groups, piece_rows, features),
        "dp",
        split_axis=0,
        concat_axis=0,
        tiled=True,
    )
    grad_in = jnp.zeros_like(x_given).at[dealing].set(returned)
    gain_pair = jnp.stack([gain_one_term, gain_two_term], axis=1)
    query_term = qkv_term[:, :head_width]
    key_term = qkv_term[:, head_width : 2 * head_width]
    value_term = qkv_term[:, 2 * head_width :]
    summed = (
        lax.psum_scatter(
            gain_pair.astype(jnp.bfloat16), "dp", scatter_dimension=0, tiled=True
        ).astype(jnp.float32),
        lax.psum_scatter(
            query_term.astype(jnp.bfloat16), "dp", scatter_dimension=0, tiled=True
        ).astype(jnp.float32),
        lax.psum_scatter(
            key_term.astype(jnp.bfloat16), "dp", scatter_dimension=0, tiled=True
        ).astype(jnp.float32),
        lax.psum_scatter(
            value_term.astype(jnp.bfloat16), "dp", scatter_dimension=0, tiled=True
        ).astype(jnp.float32),
        lax.psum_scatter(
            out_term.astype(jnp.bfloat16), "dp", scatter_dimension=0, tiled=True
        ).astype(jnp.float32),
        lax.psum_scatter(
            gate_term.astype(jnp.bfloat16), "dp", scatter_dimension=0, tiled=True
        ).astype(jnp.float32),
        lax.psum_scatter(
            up_term.astype(jnp.bfloat16), "dp", scatter_dimension=0, tiled=True
        ).astype(jnp.float32),
        lax.psum_scatter(
            down_term.astype(jnp.bfloat16), "dp", scatter_dimension=0, tiled=True
        ).astype(jnp.float32),
    )
    across = (
        lax.psum_scatter(
            jnp.tile(summed[0], (1, pieces)).astype(jnp.bfloat16),
            "tensor",
            scatter_dimension=1,
            tiled=True,
        ).astype(jnp.float32),
        lax.psum_scatter(
            summed[5].astype(jnp.bfloat16), "tensor", scatter_dimension=1, tiled=True
        ).astype(jnp.float32),
        lax.psum_scatter(
            summed[6].astype(jnp.bfloat16), "tensor", scatter_dimension=1, tiled=True
        ).astype(jnp.float32),
        lax.psum_scatter(
            summed[7].astype(jnp.bfloat16), "tensor", scatter_dimension=1, tiled=True
        ).astype(jnp.float32),
    )
    gain_sums = across[0]
    query_sum, key_sum, value_sum, out_sum = (summed[1], summed[2], summed[3], summed[4])
    gate_sum, up_sum, down_sum = (across[1], across[2], across[3])
    return (
        layer_out,
        grad_in,
        gain_sums[:, 0],
        query_sum,
        key_sum,
        value_sum,
        out_sum,
        gain_sums[:, 1],
        gate_sum,
        up_sum,
        down_sum,
    )


def solution(mesh):
    placed = (
        P(None, ("dp", "tensor"), None),
        P(),
        P(),
        P("dp"),
        P("dp", "tensor"),
        P("dp", "tensor"),
        P("dp", "tensor"),
        P("dp", "tensor"),
        P("dp"),
        P("dp", "tensor"),
        P("dp", "tensor"),
        P("dp", "tensor"),
        P("dp", None, "tensor", None, None),
    )
    return jax.shard_map(
        body,
        mesh=mesh,
        in_specs=placed,
        out_specs=(
            P("dp", None, "tensor", None, None),
            P(None, ("dp", "tensor"), None),
            P("dp"),
            P("dp", "tensor"),
            P("dp", "tensor"),
            P("dp", "tensor"),
            P("dp", "tensor"),
            P("dp"),
            P("dp", "tensor"),
            P("dp", "tensor"),
            P("dp", "tensor"),
        ),
        check_vma=False,
    )
```

profile of v0, /device:TPU:25, one launch (start us, length us, event | category | flops | bytes accessed | tf_op | source)
XLA Modules:
  0.0 1061.1 jit_solution(4126920946837255440)
XLA Ops:
  19.3 31.4 %all-reduce.3 = (bf16[768]{0:T(1024)(128)(2,1)S(1)}, bf16[768]{0:T(1024)(128)(2,1)}) all-reduce(bf16[768]{0:T(1024)(128)(2,1)S(1)} %dynamic-update-slice, bf16[768]{0:T(1024)(128)(2,1)S(1)} %dynamic-update-slice.1), channel_id=1, replica_groups=mesh['dp'=16,'tensor'=2] {'dp'}, use_global_device_ids=true, to_apply=%add | all-reduce | flops 1536 | bytes 6144
  52.8 23.1 %all_gather.44 = bf16[768,384]{1,0:T(8,128)(2,1)S(1)} all-gather(bf16[48,384]{1,0:T(8,128)(2,1)S(1)} %copy-done.47), channel_id=1, replica_groups=mesh['dp'=16,'tensor'=2] {'dp'}, dimensions={0}, use_global_device_ids=true | all-gather | bytes 626688 | tf_op jit(solution)/shard_map/all_gather | solution.py:246
  79.9 20.0 %all_gather.45 = bf16[768,384]{1,0:T(8,128)(2,1)S(1)} all-gather(bf16[48,384]{1,0:T(8,128)(2,1)S(1)} %copy-done.48), channel_id=1, replica_groups=mesh['dp'=16,'tensor'=2] {'dp'}, dimensions={0}, use_global_device_ids=true | all-gather | bytes 626688 | tf_op jit(solution)/shard_map/all_gather | solution.py:247
  100.0 19.5 %all_gather.46 = bf16[768,384]{1,0:T(8,128)(2,1)S(1)} all-gather(bf16[48,384]{1,0:T(8,128)(2,1)S(1)} %copy-done.49), channel_id=1, replica_groups=mesh['dp'=16,'tensor'=2] {'dp'}, dimensions={0}, use_global_device_ids=true | all-gather | bytes 626688 | tf_op jit(solution)/shard_map/all_gather | solution.py:248
  121.2 21.4 %all_gather.47 = bf16[768,384]{1,0:T(8,128)(2,1)} all-gather(bf16[48,384]{1,0:T(8,128)(2,1)S(1)} %copy-done.50), channel_id=1, replica_groups=mesh['dp'=16,'tensor'=2] {'dp'}, dimensions={0}, use_global_device_ids=true | all-gather | bytes 626688 | tf_op jit(solution)/shard_map/all_gather | solution.py:249
  158.8 26.6 %while.71 = (s32[]{:T(128)}, f32[1024,8,48]{0,2,1:T(8,128)}, f32[8,1024]{1,0:T(8,128)}, s32[]{:T(128)}, bf16[1024,8,48]{0,2,1:T(8,128)(2,1)}, /*index=5*/bf16[10...) while((s32[]{:T(128)}, f32[1024,8,48]{0,2,1:T(8,128)}, ...), condition=%wide.region_8.9_spmd, body=%wide.region_1.8_spmd.sunk | while | flops 627783680 | bytes 25118492 | solution.py:137
  219.6 9.8 reduce-scatter.16.cloned.1.call-done
  233.7 22.0 %all-gather.7.cloned.1.call-done = bf16[768,2560]{1,0:T(8,128)(2,1)} async-done(((bf16[48,2560]{1,0:T(8,128)(2,1)}), bf16[768,2560]{1,0:T(8,128)(2,1)}) %all-gather.7.cloned.1.call-update) | async-done | bytes 3932176 | tf_op jit(solution)/shard_map/all_gather | solution.py:250
  262.3 43.5 %all-gather.9.cloned.1.call-done = bf16[768,2560]{1,0:T(8,128)(2,1)} async-done(((bf16[48,2560]{1,0:T(8,128)(2,1)}), bf16[768,2560]{1,0:T(8,128)(2,1)}) %all-gather.9.cloned.1.call-update) | async-done | bytes 3932176 | tf_op jit(solution)/shard_map/all_gather | solution.py:251
  312.5 43.4 %all-gather.11.cloned.1.call-done = bf16[768,2560]{1,0:T(8,128)(2,1)} async-done(((bf16[48,2560]{1,0:T(8,128)(2,1)}), bf16[768,2560]{1,0:T(8,128)(2,1)}) %all-gather.11.cloned.1.call-update) | async-done | bytes 3932176 | tf_op jit(solution)/shard_map/all_gather | solution.py:252
  374.1 26.9 %all-gather.13.cloned.1.call-done = bf16[16,2,32,768]{3,2,1,0:T(8,128)(2,1)} async-done(((bf16[16,1,32,768]{3,2,1,0:T(8,128)(2,1)}), bf16[16,2,32,768]{3,2,1,0:T(8,128)(2,1)}) %all-gather.13.cloned.1.call-update) | async-done | bytes 1572880 | tf_op jit(solution)/shard_map/all_gather | solution.py:320
  409.2 42.0 %while.73 = (s32[]{:T(128)}, f32[1024,8,48]{0,2,1:T(8,128)}, f32[1024,8,48]{0,2,1:T(8,128)S(1)}, f32[1024,8,48]{0,2,1:T(8,128)}, s32[]{:T(128)}, /*index=5*/f32[...) while((s32[]{:T(128)}, f32[1024,8,48]{0,2,1:T(8,128)}, ...), condition=%wide.region_15.16_spmd, body=%wide.region_12.15_spmd.sunk | while | flops 1028850688 | bytes 54846124 | solution.py:198
  412.9 10.9 %while.76 = (s32[]{:T(128)}, f32[512,8,48]{0,2,1:T(8,128)S(1)}, f32[1024,8,48]{0,2,1:T(8,128)S(1)}, f32[1024,8,48]{0,2,1:T(8,128)}, s32[]{:T(128)}, /*index=5*/b...) while((s32[]{:T(128)}, f32[512,8,48]{0,2,1:T(8,128)S(1)}, ...), condition=%wide.region_14.14_spmd, body=%wide.region_13.13_spmd.sunk | while | flops 1028850688 | bytes 50848048 | solution.py:193
  428.2 21.8 %while.76 = (s32[]{:T(128)}, f32[512,8,48]{0,2,1:T(8,128)S(1)}, f32[1024,8,48]{0,2,1:T(8,128)S(1)}, f32[1024,8,48]{0,2,1:T(8,128)}, s32[]{:T(128)}, /*index=5*/b...) while((s32[]{:T(128)}, f32[512,8,48]{0,2,1:T(8,128)S(1)}, ...), condition=%wide.region_14.14_spmd, body=%wide.region_13.13_spmd.sunk | while | flops 1028850688 | bytes 50848048 | solution.py:193
  508.2 65.7 %reduce-scatter.32.cloned.1.call-done = bf16[48,2560]{1,0:T(8,128)(2,1)} async-done(((bf16[768,2560]{1,0:T(8,128)(2,1)}), bf16[48,2560]{1,0:T(8,128)(2,1)}) %reduce-scatter.32.cloned.1.call-update) | async-done | bytes 245776 | tf_op jit(solution)/shard_map/reduce_scatter | solution.py:387
  574.0 73.5 %reduce-scatter.36.cloned.1.call-done = bf16[48,2560]{1,0:T(8,128)(2,1)} async-done(((bf16[768,2560]{1,0:T(8,128)(2,1)}), bf16[48,2560]{1,0:T(8,128)(2,1)}) %reduce-scatter.36.cloned.1.call-update) | async-done | bytes 245776 | tf_op jit(solution)/shard_map/reduce_scatter | solution.py:390
  659.5 45.0 %reduce-scatter.26.cloned.1.call-done = bf16[48,384]{1,0:T(8,128)(2,1)} async-done(((bf16[768,384]{1,0:T(8,128)(2,1)}), bf16[48,384]{1,0:T(8,128)(2,1)}) %reduce-scatter.26.cloned.1.call-update) | async-done | bytes 36880 | tf_op jit(solution)/shard_map/reduce_scatter | solution.py:381
  705.9 56.5 %reduce-scatter.20.cloned.1.call-done = bf16[48,384]{1,0:T(8,128)(2,1)} async-done(((bf16[768,384]{1,0:T(8,128)(2,1)}), bf16[48,384]{1,0:T(8,128)(2,1)}) %reduce-scatter.20.cloned.1.call-update) | async-done | bytes 36880 | tf_op jit(solution)/shard_map/reduce_scatter | solution.py:372
  763.8 56.1 %reduce-scatter.22.cloned.1.call-done = bf16[48,384]{1,0:T(8,128)(2,1)} async-done(((bf16[768,384]{1,0:T(8,128)(2,1)}), bf16[48,384]{1,0:T(8,128)(2,1)}) %reduce-scatter.22.cloned.1.call-update) | async-done | bytes 36880 | tf_op jit(solution)/shard_map/reduce_scatter | solution.py:375
  821.3 56.9 %reduce-scatter.24.cloned.1.call-done = bf16[48,384]{1,0:T(8,128)(2,1)} async-done(((bf16[768,384]{1,0:T(8,128)(2,1)}), bf16[48,384]{1,0:T(8,128)(2,1)}) %reduce-scatter.24.cloned.1.call-update) | async-done | bytes 36880 | tf_op jit(solution)/shard_map/reduce_scatter | solution.py:378
  879.6 72.3 %reduce-scatter.28.cloned.1.call-done = bf16[48,2560]{1,0:T(8,128)(2,1)} async-done(((bf16[768,2560]{1,0:T(8,128)(2,1)}), bf16[48,2560]{1,0:T(8,128)(2,1)}) %reduce-scatter.28.cloned.1.call-update) | async-done | bytes 245776 | tf_op jit(solution)/shard_map/reduce_scatter | solution.py:384
  958.0 50.6 %reduce-scatter.40.cloned.1.call-done = bf16[48,2]{1,0:T(8,128)(2,1)} async-done(((bf16[768,2]{1,0:T(8,128)(2,1)}), bf16[48,2]{1,0:T(8,128)(2,1)}) %reduce-scatter.40.cloned.1.call-update) | async-done | bytes 208
  1026.1 12.1 %reduce-scatter.38.cloned.1.call-done = bf16[48,1280]{1,0:T(8,128)(2,1)} async-done(((bf16[48,2560]{1,0:T(8,128)(2,1)}), bf16[48,1280]{1,0:T(8,128)(2,1)}) %reduce-scatter.38.cloned.1.call-update) | async-done | bytes 122896 | tf_op jit(solution)/shard_map/reduce_scatter | solution.py:407
  1039.8 12.1 %reduce-scatter.30.cloned.1.call-done = bf16[48,1280]{1,0:T(8,128)(2,1)} async-done(((bf16[48,2560]{1,0:T(8,128)(2,1)}), bf16[48,1280]{1,0:T(8,128)(2,1)}) %reduce-scatter.30.cloned.1.call-update) | async-done | bytes 122896 | tf_op jit(solution)/shard_map/reduce_scatter | solution.py:401
  (367 shorter events, 297.9 us)
Async XLA Ops:
  11.1 39.6 %all-to-all-start = ((bf16[16,32,768]{2,1,0:T(8,128)(2,1)}), bf16[16,32,768]{2,1,0:T(8,128)(2,1)S(1)}, u32[]{:S(2)}, u32[]{:S(2)}) async-start(bf16[16,32,768]{2,1,0:T(8,128)(2,1)} %broadcast_select_fusion), calls=%async_computation | async-start | bytes 1572864 | tf_op jit(solution)/shard_map/all_to_all | solution.py:231
  17.5 125.1 %all-gather.15.cloned.1.call-start = ((), (), s32[]{:S(2)}) async-start(), calls=%async_computation.31 | async-start | bytes 2359296 | tf_op jit(solution)/shard_map/all_gather | solution.py:268
  52.8 176.7 %reduce-scatter.16.cloned.1.call-start = ((), (), s32[]{:S(2)}) async-start(), calls=%async_computation.15 | async-start | bytes 2359296 | tf_op jit(solution)/shard_map/reduce_scatter | solution.py:289
  197.0 58.7 %all-gather.7.cloned.1.call-start = ((), (), s32[]{:S(2)}) async-start(), calls=%async_computation.16 | async-start | bytes 4177920 | tf_op jit(solution)/shard_map/all_gather | solution.py:250
  202.7 103.1 %all-gather.9.cloned.1.call-start = ((), (), s32[]{:S(2)}) async-start(), calls=%async_computation.17 | async-start | bytes 4177920 | tf_op jit(solution)/shard_map/all_gather | solution.py:251
  210.0 145.9 %all-gather.11.cloned.1.call-start = ((), (), s32[]{:S(2)}) async-start(), calls=%async_computation.18 | async-start | bytes 4177920 | tf_op jit(solution)/shard_map/all_gather | solution.py:252
  218.7 182.3 %all-gather.13.cloned.1.call-start = ((), (), s32[]{:S(2)}) async-start(), calls=%async_computation.19 | async-start | bytes 2359296 | tf_op jit(solution)/shard_map/all_gather | solution.py:320
  219.0 153.3 %copy-start.43 = (f32[768]{0:T(1024)}, f32[768]{0:T(1024)S(1)}, u32[]{:S(2)}) copy-start(f32[768]{0:T(1024)S(1)} %convert_element_type.202) | copy-start | bytes 9220
  219.6 152.7 %copy-start.45 = (f32[512]{0:T(512)}, f32[512]{0:T(512)S(1)}, u32[]{:S(2)}) copy-start(f32[512]{0:T(512)S(1)} %fusion.86) | copy-start | bytes 6148
  374.0 131.1 %reduce-scatter.18.cloned.1.call-start = ((), (), s32[]{:S(2)}) async-start(), calls=%async_computation.20 | async-start | bytes 2359296 | tf_op jit(solution)/shard_map/reduce_scatter | solution.py:348
  477.2 96.8 %reduce-scatter.32.cloned.1.call-start = ((), (), s32[]{:S(2)}) async-start(), calls=%async_computation.27 | async-start | bytes 4177920 | tf_op jit(solution)/shard_map/reduce_scatter | solution.py:387
  481.4 166.1 %reduce-scatter.36.cloned.1.call-start = ((), (), s32[]{:S(2)}) async-start(), calls=%async_computation.29 | async-start | bytes 4177920 | tf_op jit(solution)/shard_map/reduce_scatter | solution.py:390
  488.8 215.7 %reduce-scatter.26.cloned.1.call-start = ((), (), s32[]{:S(2)}) async-start(), calls=%async_computation.24 | async-start | bytes 626688 | tf_op jit(solution)/shard_map/reduce_scatter | solution.py:381
  493.3 269.1 %reduce-scatter.20.cloned.1.call-start = ((), (), s32[]{:S(2)}) async-start(), calls=%async_computation.21 | async-start | bytes 626688 | tf_op jit(solution)/shard_map/reduce_scatter | solution.py:372
  498.7 321.2 %reduce-scatter.22.cloned.1.call-start = ((), (), s32[]{:S(2)}) async-start(), calls=%async_computation.22 | async-start | bytes 626688 | tf_op jit(solution)/shard_map/reduce_scatter | solution.py:375
  499.5 378.7 %reduce-scatter.24.cloned.1.call-start = ((), (), s32[]{:S(2)}) async-start(), calls=%async_computation.23 | async-start | bytes 626688 | tf_op jit(solution)/shard_map/reduce_scatter | solution.py:378
  500.1 451.9 %reduce-scatter.28.cloned.1.call-start = ((), (), s32[]{:S(2)}) async-start(), calls=%async_computation.25 | async-start | bytes 4177920 | tf_op jit(solution)/shard_map/reduce_scatter | solution.py:384
  504.3 143.3 %copy-start.7 = (bf16[512,768]{1,0:T(8,128)(2,1)S(1)}, bf16[512,768]{1,0:T(8,128)(2,1)}, u32[]{:S(2)}) copy-start(bf16[512,768]{1,0:T(8,128)(2,1)} %reduce-scatter.16.cloned.1.call-done) | copy-start | bytes 2359300
  504.4 504.2 %reduce-scatter.40.cloned.1.call-start = ((), (), s32[]{:S(2)}) async-start(), calls=%async_computation.32 | async-start | bytes 208896
  508.2 516.3 %reduce-scatter.34.cloned.1.call-start = ((), (), s32[]{:S(2)}) async-start(), calls=%async_computation.28 | async-start | bytes 368640 | tf_op jit(solution)/shard_map/reduce_scatter | solution.py:404
  574.0 464.2 %reduce-scatter.38.cloned.1.call-start = ((), (), s32[]{:S(2)}) async-start(), calls=%async_computation.30 | async-start | bytes 368640 | tf_op jit(solution)/shard_map/reduce_scatter | solution.py:407
  650.9 301.0 %copy-start.23 = (f32[512,768]{1,0:T(8,128)S(1)}, f32[512,768]{1,0:T(8,128)}, u32[]{:S(2)}) copy-start(f32[512,768]{1,0:T(8,128)} %get-tuple-element.696) | copy-start | bytes 4718596
  650.9 362.8 %all-to-all-start.1 = ((bf16[16,32,768]{2,1,0:T(8,128)(2,1)}), bf16[16,32,768]{2,1,0:T(8,128)(2,1)S(1)}, u32[]{:S(2)}, u32[]{:S(2)}) async-start(bf16[16,32,768]{2,1,0:T(8,128)(2,1)} %bitcast.207), calls=%async_computation.3 | async-start | bytes 1572864 | tf_op jit(solution)/shard_map/all_to_all | solution.py:356
  658.2 393.6 %reduce-scatter.30.cloned.1.call-start = ((), (), s32[]{:S(2)}) async-start(), calls=%async_computation.26 | async-start | bytes 368640 | tf_op jit(solution)/shard_map/reduce_scatter | solution.py:401
  (71 other events, 1735.3 us)
Sparse Core Ops, SparseCore 0:
  52.9 32.1 all-gather.14
  197.1 32.3 reduce-scatter.15
  374.1 26.7 all-gather.12
  477.3 25.1 reduce-scatter.17
  506.2 67.6 reduce-scatter.31
  578.2 69.3 reduce-scatter.35
  651.1 53.3 reduce-scatter.25
  708.5 53.8 reduce-scatter.19
  766.0 53.8 reduce-scatter.21
  824.3 53.8 reduce-scatter.23
  882.1 69.7 reduce-scatter.27
  956.3 52.2 reduce-scatter.39
  1010.9 13.5 reduce-scatter.33
  1026.7 11.4 reduce-scatter.37
  1040.4 11.4 reduce-scatter.29
Sparse Core Ops, SparseCore 1:
  202.8 52.8 all-gather.6
  258.1 47.7 all-gather.8
  308.3 47.7 all-gather.10
where the time goes:
time: 1070 us; the launch traced here: 1060 us
  waiting for transfers between devices  657 us (61%)
  blocking collectives  141 us (13%)
  matrix products  114 us (11%)
  local copies, waits for them, and re-layouts  62.3 us (6%)
  other arithmetic  49.6 us (5%)
  between operations  20.7 us (2%)
  starting transfers between devices  14.8 us (1%)
    reduce_scatter x1, waiting for transfers between devices, body(): lax.psum_scatter(down_term.astype(jnp.bfloat16), 'dp', scatter_dimension=...  73.5 us
    reduce_scatter x1, waiting for transfers between devices, body(): lax.psum_scatter(gate_term.astype(jnp.bfloat16), 'dp', scatter_dimension=...  72.3 us
    reduce_scatter x1, waiting for transfers between devices, body(): lax.psum_scatter(up_term.astype(jnp.bfloat16), 'dp', scatter_dimension=0,...  65.7 us
    reduce_scatter x1, waiting for transfers between devices, body(): lax.psum_scatter(value_term.astype(jnp.bfloat16), 'dp', scatter_dimension...  56.9 us
    reduce_scatter x1, waiting for transfers between devices, body(): lax.psum_scatter(query_term.astype(jnp.bfloat16), 'dp', scatter_dimension...  56.5 us
    reduce_scatter x1, waiting for transfers between devices, body(): lax.psum_scatter(key_term.astype(jnp.bfloat16), 'dp', scatter_dimension=0...  56.1 us
    unnamed x19, waiting for transfers between devices  52.1 us
    reduce_scatter x1, waiting for transfers between devices, body(): lax.psum_scatter(out_term.astype(jnp.bfloat16), 'dp', scatter_dimension=0...  45 us
  transfers between devices with their start and end apart: 20, of which 16 were waited for; matrix products, arithmetic and copies ran while one was open for 6% of the time, Pallas kernels for 0%

commit v1 on v0

--- a/solution.py
+++ b/solution.py
@@ -1,6 +1,11 @@
+import functools
+
 import jax
 import jax.numpy as jnp
+import numpy as np
 from jax import lax
+from jax.experimental import pallas as pl
+from jax.experimental.pallas import tpu as pltpu
 from jax.sharding import PartitionSpec as P
 
 HD = 48
@@ -8,6 +13,7 @@
 
 EPS = 1e-05
 BASE = 10000.0
+VMEM_LIMIT = 64 * 1024 * 1024 - 65536
 
 
 def tables(positions, head_size):
@@ -426,6 +432,938 @@
     )
 
 
+MESH = pl.DeviceIdType.MESH
+BF = jnp.bfloat16
+F32 = jnp.float32
+NN = (((1,), (0,)), ((), ()))
+NT = (((1,), (1,)), ((), ()))
+TN = (((0,), (0,)), ((), ()))
+LOG2E = 1.4426950408889634
+ROWS = 256
+
+
+def mm(kind, left_side, right_side):
+    return lax.dot_general(left_side, right_side, kind, preferred_element_type=F32)
+
+
+def fused_kernel(
+    shape,
+    deal, lens, x_ref, dy_ref, g1, g2, wq, wk, wv, wo, wg, wu, wd, tab,
+    lo_ref, gi_ref, dq_out, dk_out, dv_out, do_out, dg_out, du_out, dd_out, dgain_out,
+    xs, xbuf, dybuf, src_a, src_f, w_a, w_o, w_f, wp, wop, eqk, ev, cosb, sinb, ct, st,
+    abuf, qb, kb, vb, vt, ot, ob, lse, own, sb1, sb2, rb1, rb2, x1b, r1b, r2b, bbuf, dfb,
+    facc, uacc, act, dob, delta, rx_a, ry_a, ry2_a, rz_a, rx_o, ry_o, ry2_o, rz_o,
+    rx_f, ry_f, ry2_f, rz_f, ret, gs, gr, rsum,
+    a2a_s, a2a_r, dy_s, dy_r, ag_z, ag_x, ag_y, ag_d, ag_s, rs_x, rs_y, rs_z, rs_s,
+    ex_s, ex_r, lo_s, lo_r, ret_s, ret_r, gg_s, gg_r,
+):
+    nz, nf, dim, hw, chunk, nrow = shape
+    groups = 4 * nz
+    seq_len = 64 * groups
+    half = dim // 2
+    nrb = seq_len // ROWS
+    kd = nz // 2
+    dp = lax.axis_index("dp")
+    y = lax.axis_index("tensor")
+    z = dp // 4
+    x = (dp // 2) % 2
+    c = dp % 2
+    xb, yb, oth = 1 - x, 1 - y, 1 - c
+    home = c == y
+    away = c != y
+    slot = (z * 2 + x) * 2 + y
+    score_scale = HD ** (-0.5)
+
+    def dev(z_, x_, c_, y_):
+        return ((z_ * 2 + x_) * 2 + c_, y_)
+
+    partner = dev(z, x, oth, y)
+    xnbr = dev(z, xb, c, y)
+    ynbr = dev(z, x, c, yb)
+    swap = dev(z, x, oth, yb)
+
+    def rc(src, dst, ss, rs, to):
+        return pltpu.make_async_remote_copy(
+            src_ref=src, dst_ref=dst, send_sem=ss, recv_sem=rs, device_id=to, device_id_type=MESH
+        )
+
+    def wait(ref, sem):
+        pltpu.make_async_copy(ref, ref, sem).wait()
+
+    bar = pltpu.get_barrier_semaphore()
+    ndev = groups * 2
+
+    def greet(i, _):
+        t = lax.rem(dp * 2 + y + i, ndev)
+        pl.semaphore_signal(bar, inc=1, device_id=(t // 2, t % 2), device_id_type=MESH)
+        return 0
+
+    lax.fori_loop(1, ndev, greet, 0)
+    pl.semaphore_wait(bar, ndev - 1)
+
+    def stage(j, _):
+        xs[j] = x_ref[deal[j]]
+        return 0
+
+    lax.fori_loop(0, groups, stage, 0)
+
+    def deal_out(i, _):
+        j = lax.rem(slot + i, groups)
+        dpd = (j // 2) * 2 + y
+        td = j % 2
+        same = (dpd == dp) & (td == y)
+
+        @pl.when(same)
+        def _():
+            pltpu.make_async_copy(xs.at[j], xbuf.at[dp], a2a_r).start()
+
+        @pl.when(jnp.logical_not(same))
+        def _():
+            rc(xs.at[j], xbuf.at[dp], a2a_s, a2a_r, (dpd, td)).start()
+
+        return 0
+
+    lax.fori_loop(0, groups, deal_out, 0)
+
+    def unit(k):
+        if isinstance(k, str):
+            return (src_a, w_a, 0) if k == "a" else (wo, w_o, 1)
+        return (src_f.at[k], w_f.at[k], k + 2)
+
+    def zsend(k):
+        src, buf, n = unit(k)
+        for i in range(1, nz):
+            zt = lax.rem(z + i, nz)
+            rc(src, buf.at[z, x, c], ag_s.at[n, i - 1], ag_z.at[n], dev(zt, x, y, y)).start()
+
+        @pl.when(home)
+        def _():
+            pltpu.make_async_copy(src, buf.at[z, x, c], ag_z.at[n]).start()
+
+        @pl.when(away)
+        def _():
+            rc(src, buf.at[z, x, c], ag_s.at[n, nz - 1], ag_z.at[n], dev(z, x, y, y)).start()
+
+    def ag1(k):
+        src, buf, n = unit(k)
+
+        @pl.when(home)
+        def _():
+            wait(buf.at[:, x], ag_z.at[n])
+            rc(buf.at[:, x], buf.at[:, x], ag_s.at[n, nz], ag_y.at[n], ynbr).start()
+            rc(buf.at[:, x], buf.at[:, x], ag_s.at[n, nz + 1], ag_x.at[n], xnbr).start()
+
+    def ag2(k):
+        src, buf, n = unit(k)
+
+        @pl.when(home)
+        def _():
+            wait(buf.at[:, xb], ag_x.at[n])
+            part = buf.at[pl.ds(0, kd), xb]
+            rc(part, part, ag_s.at[n, nz + 2], ag_d.at[n, 0], ynbr).start()
+
+        @pl.when(away)
+        def _():
+            wait(buf.at[:, x], ag_y.at[n])
+            part = buf.at[pl.ds(kd, nz - kd), x]
+            rc(part, part, ag_s.at[n, nz + 2], ag_d.at[n, 1], xnbr).start()
+
+    def ag3(k):
+        src, buf, n = unit(k)
+
+        @pl.when(away)
+        def _():
+            wait(buf.at[pl.ds(0, kd), xb], ag_d.at[n, 0])
+            wait(buf.at[pl.ds(kd, nz - kd), xb], ag_d.at[n, 1])
+
+    def ag_done(k):
+        src, buf, n = unit(k)
+        for i in range(nz - 1):
+            wait(src, ag_s.at[n, i])
+
+        @pl.when(home)
+        def _():
+            wait(buf.at[:, x], ag_s.at[n, nz])
+            wait(buf.at[:, x], ag_s.at[n, nz + 1])
+            wait(buf.at[pl.ds(0, kd), xb], ag_s.at[n, nz + 2])
+
+        @pl.when(away)
+        def _():
+            wait(src, ag_s.at[n, nz - 1])
+            wait(buf.at[pl.ds(kd, nz - kd), x], ag_s.at[n, nz + 2])
+
+    def rs_unit(k):
+        if isinstance(k, str):
+            if k == "a":
+                return (w_a, rx_a, ry_a, ry2_a, rz_a, 0)
+            return (w_o, rx_o, ry_o, ry2_o, rz_o, 1)
+        return (w_f.at[k], rx_f.at[k], ry_f.at[k], ry2_f.at[k], rz_f.at[k], k + 2)
+
+    lo_z = pl.ds(0, kd)
+    hi_z = pl.ds(kd, nz - kd)
+
+    def at_unit(ref, k, *spot):
+        spot = spot if isinstance(k, str) else (k,) + spot
+        return ref[spot if spot else ...].astype(F32)
+
+    def put_unit(ref, k, total, *spot):
+        spot = spot if isinstance(k, str) else (k,) + spot
+        ref[spot if spot else ...] = total.astype(BF)
+
+    def rs_refs(k):
+        if isinstance(k, str):
+            return (w_a, rx_a, ry_a, ry2_a) if k == "a" else (w_o, rx_o, ry_o, ry2_o)
+        return w_f, rx_f, ry_f, ry2_f
+
+    every = slice(None)
+
+    def by_x(step):
+        for v in range(2):
+            pl.when(x == v)(functools.partial(step, v, 1 - v))
+
+    def rs0(k):
+        g, rx, ry, ry2, rz, n = rs_unit(k)
+        rc(g.at[hi_z, xb], rx.at[hi_z], rs_s.at[n, 0], rs_x.at[n, 1], xnbr).start()
+
+        @pl.when(away)
+        def _():
+            rc(g.at[lo_z], ry, rs_s.at[n, 1], rs_y.at[n, 0], ynbr).start()
+
+    def rs1(k):
+        g, rx, ry, ry2, rz, n = rs_unit(k)
+        g_all, rx_all, ry_all, ry2_all = rs_refs(k)
+
+        @pl.when(away)
+        def _():
+            wait(rx.at[hi_z], rs_x.at[n, 1])
+
+            @by_x
+            def _(v, vb):
+                put_unit(ry2_all, k, at_unit(g_all, k, hi_z, v) + at_unit(rx_all, k, hi_z))
+
+            rc(ry2, ry2, rs_s.at[n, 2], rs_y.at[n, 1], ynbr).start()
+
+        @pl.when(home)
+        def _():
+            wait(ry, rs_y.at[n, 0])
+
+            @by_x
+            def _(v, vb):
+                total = at_unit(g_all, k, lo_z, vb) + at_unit(ry_all, k, every, vb)
+                put_unit(ry_all, k, total, every, vb)
+
+            rc(ry.at[:, xb], rx.at[lo_z], rs_s.at[n, 2], rs_x.at[n, 0], xnbr).start()
+
+    def rs2(k):
+        g, rx, ry, ry2, rz, n = rs_unit(k)
+        g_all, rx_all, ry_all, ry2_all = rs_refs(k)
+
+        @pl.when(home)
+        def _():
+            wait(rx.at[hi_z], rs_x.at[n, 1])
+            wait(ry2, rs_y.at[n, 1])
+
+            @by_x
+            def _(v, vb):
+                total = at_unit(g_all, k, hi_z, v) + at_unit(rx_all, k, hi_z) + at_unit(ry2_all, k)
+                put_unit(rx_all, k, total, hi_z)
+
+            wait(rx.at[lo_z], rs_x.at[n, 0])
+
+            @by_x
+            def _(v, vb):
+                total = at_unit(g_all, k, lo_z, v) + at_unit(ry_all, k, every, v)
+                put_unit(rx_all, k, total + at_unit(rx_all, k, lo_z), lo_z)
+
+            for i in range(1, nz):
+                zt = lax.rem(z + i, nz)
+                for cc in range(2):
+                    rc(
+                        rx.at[zt, cc], rz.at[z], rs_s.at[n, 3 + 2 * (i - 1) + cc], rs_z.at[n],
+                        dev(zt, x, cc, y),
+                    ).start()
+            rc(rx.at[z, oth], rz.at[z], rs_s.at[n, 2 * nz + 1], rs_z.at[n], partner).start()
+            pltpu.make_async_copy(rx.at[z, c], rz.at[z], rs_z.at[n]).start()
+
+    def rs_done(k):
+        g, rx, ry, ry2, rz, n = rs_unit(k)
+        wait(rx.at[hi_z], rs_s.at[n, 0])
+
+        @pl.when(away)
+        def _():
+            wait(ry, rs_s.at[n, 1])
+            wait(ry2, rs_s.at[n, 2])
+
+        @pl.when(home)
+        def _():
+            wait(rx.at[lo_z], rs_s.at[n, 2])
+            for i in range(2 * (nz - 1) + 1):
+                wait(rz.at[0], rs_s.at[n, 3 + i])
+
+    def rs3(k):
+        g, rx, ry, ry2, rz, n = rs_unit(k)
+        wait(rz, rs_z.at[n])
+        total = None
+        for i in range(nz):
+            part = (rz[i] if isinstance(k, str) else rz_f[k, i]).astype(F32)
+            total = part if total is None else total + part
+        return total
+
+    gain1 = g1[...]
+    gain2 = g2[...]
+    for i, w in enumerate((wq, wk, wv)):
+        src_a[:, i * hw : (i + 1) * hw] = (w[...].astype(F32) * gain1).astype(BF)
+    zsend("a")
+    zsend("o")
+
+    @pl.when(home)
+    def _():
+        pltpu.make_async_copy(dy_ref, dybuf, dy_r).start()
+
+    @pl.when(away)
+    def _():
+        rc(dy_ref, dybuf, dy_s, dy_r, swap).start()
+
+    for f in range(nf):
+        cols = slice(f * chunk, (f + 1) * chunk)
+        src_f[f, :, 0:chunk] = (wg[:, cols].astype(F32) * gain2).astype(BF)
+        src_f[f, :, chunk : 2 * chunk] = (wu[:, cols].astype(F32) * gain2).astype(BF)
+        src_f[f, :, 2 * chunk : 3 * chunk] = wd[:, cols]
+
+    def rope_rows(i, _):
+        ca, sa = tab[0, pl.ds(i, 1), :], tab[1, pl.ds(i, 1), :]
+        cb, sb = tab[2], tab[3]
+        at = pl.ds(pl.multiple_of(i * 32, 32), 32)
+        cosb[at, :] = ca * cb - sa * sb
+        sinb[at, :] = sa * cb + ca * sb
+        return 0
+
+    lax.fori_loop(0, seq_len // 32, rope_rows, 0)
+    for i in range(nrb):
+        at = slice(i * ROWS, (i + 1) * ROWS)
+        ct[:, at] = cosb[at, :].T[0:32]
+        st[:, at] = sinb[at, :].T[0:32]
+    pw = wop.shape[1]
+    row = lax.broadcasted_iota(jnp.int32, (hw, pw), 0)
+    col = lax.broadcasted_iota(jnp.int32, (hw, pw), 1)
+    low = col & 31
+    spot = ((col >> 8) * 4 + ((col >> 5) & 3)) * HD + ((col >> 7) & 1) * (HD // 2) + low
+    eqk[...] = jnp.where((row == spot) & (low < HD // 2), 1.0, 0.0).astype(BF)
+    low = col & 63
+    ev[...] = jnp.where((row == (col >> 6) * HD + low) & (low < HD), 1.0, 0.0).astype(BF)
+    facc[...] = jnp.zeros_like(facc)
+    uacc[...] = jnp.zeros_like(uacc)
+
+    length = lens[deal[slot]]
+
+    def live_at(i):
+        at = (i * 2 + c) * 32 + lax.broadcasted_iota(jnp.int32, (32, 1), 0)
+        return at < length
+
+    def mean(values):
+        return jnp.mean(values, axis=1, keepdims=True)
+
+    def swap_start(n, src, dst):
+        rc(src, dst, ex_s.at[n], ex_r.at[n], partner).start()
+
+    def blk(i):
+        return pl.ds(i * (ROWS // 64), ROWS // 64)
+
+    ag1("a")
+    ag1("o")
+    zsend(0)
+    zsend(1)
+    wait(xbuf, a2a_r)
+    wait(dybuf, dy_r)
+
+    def norm_one(i, _):
+        rows_now = xbuf[i].astype(F32)
+        r = lax.rsqrt(mean(rows_now * rows_now) + EPS)
+        r1b[i] = jnp.broadcast_to(r, (32, 128))
+        abuf[i, c] = (rows_now * r).astype(BF)
+        dfb[i, c] = jnp.where(live_at(i), dybuf[i], jnp.zeros((32, dim), BF))
+        return 0
+
+    lax.fori_loop(0, groups, norm_one, 0, unroll=2)
+    swap_start(0, abuf.at[:, c], abuf.at[:, c])
+    swap_start(1, dfb.at[:, c], dfb.at[:, c])
+    ag2("a")
+    ag1(0)
+    ag3("a")
+    for i in range(3):
+        e = eqk if i < 2 else ev
+        wp[:, i * pw : (i + 1) * pw] = mm(
+            NN, w_a[:, :, :, :, i * hw : (i + 1) * hw].reshape(dim, hw), e[...]
+        ).astype(BF)
+    wait(abuf.at[:, oth], ex_r.at[0])
+
+    query_scale = score_scale * LOG2E
+    lane64 = lax.broadcasted_iota(jnp.int32, (ROWS, pw), 1) & 63
+
+    def project(i, _):
+        a = abuf[blk(i)].reshape(ROWS, dim)
+        at = pl.ds(pl.multiple_of(i * ROWS, ROWS), ROWS)
+        cos, sin = cosb[at, :], sinb[at, :]
+        for t, (dst, scale) in enumerate(((qb, query_scale), (kb, 1.0))):
+            u = mm(NN, a, wp[:, t * pw : (t + 1) * pw]) * scale
+            for g in range(pw // 256):
+                f1 = u[:, g * 256 : g * 256 + 128]
+                f2 = u[:, g * 256 + 128 : g * 256 + 256]
+                dst[blk(i), :, :, g * 256 : g * 256 + 128] = (
+                    (f1 * cos - f2 * sin).astype(BF).reshape(ROWS // 64, 2, 32, 128)
+                )
+                dst[blk(i), :, :, g * 256 + 128 : g * 256 + 256] = (
+                    (f2 * cos + f1 * sin).astype(BF).reshape(ROWS // 64, 2, 32, 128)
+                )
+        v = mm(NN, a, wp[:, 2 * pw : 3 * pw])
+        v = jnp.where(lane64 == HD, 1.0, v).astype(BF)
+        vb[blk(i)] = v.reshape(ROWS // 64, 2, 32, pw)
+        vt[:, at] = v.T
+        return 0
+
+    lax.fori_loop(0, nrb, project, 0)
+    zsend(2)
+    ag1(1)
+    ag2("o")
+
+    lane = lax.broadcasted_iota(jnp.int32, (ROWS, 256), 1)
+    diag = lax.broadcasted_iota(jnp.int32, (ROWS, ROWS), 0) <= lax.broadcasted_iota(
+        jnp.int32, (ROWS, ROWS), 1
+    )
+
+    def rows_of(ref, first, count, lanes):
+        return ref[pl.ds(first // 64, count // 64), :, :, lanes].reshape(count, 256)
+
+    def attend(i):
+        keys = (i + 1) * ROWS
+
+        def group(g, _):
+            lanes = pl.ds(pl.multiple_of(g * 256, 256), 256)
+            q = rows_of(qb, i * ROWS, ROWS, lanes)
+            for hh in range(4):
+                qm = jnp.where(((lane >> 5) & 3) == hh, q, jnp.zeros_like(q))
+                sd = mm(NT, rows_of(kb, i * ROWS, ROWS, lanes), qm)
+                sd = jnp.where(diag, sd, -1e30)
+                top = jnp.max(sd, axis=0, keepdims=True)
+                if i:
+                    s = mm(NT, rows_of(kb, 0, i * ROWS, lanes), qm)
+                    top = jnp.maximum(top, jnp.max(s, axis=0, keepdims=True))
+                    p = jnp.concatenate(
+                        [jnp.exp2(s - top).astype(BF), jnp.exp2(sd - top).astype(BF)], axis=0
+                    )
+                else:
+                    p = jnp.exp2(sd - top).astype(BF)
+                hs = pl.multiple_of(g * 256 + hh * 64, 64)
+                o = mm(NN, vt[pl.ds(hs, 64), 0:keys], p)
+                total = o[HD : HD + 1, :]
+                ot[pl.ds(hs, 64), i * ROWS : keys] = (o * (1.0 / total)).astype(BF)
+                lse[pl.ds(g * 4 + hh, 1), i * ROWS : keys] = top + jnp.log2(total)
+            return 0
+
+        lax.fori_loop(0, pw // 256, group, 0)
+
+    def during_one():
+        ag2(0)
+        ag3("o")
+        wop[...] = mm(NN, w_o[...].reshape(dim, hw), ev[...]).astype(BF)
+        ag1(2)
+        zsend(3)
+        zsend(4)
+
+    def during_two():
+        ag2(1)
+        ag1(3)
+
+    def with_steps(part, steps):
+        for i in range(nrb):
+            part(i)
+            for at, step in steps:
+                if min(at, nrb - 1) == i:
+                    step()
+
+    with_steps(attend, ((1, during_one), (2, during_two)))
+
+    def turn(i, _):
+        at = pl.ds(pl.multiple_of(i * ROWS, ROWS), ROWS)
+        ob[blk(i)] = ot[:, at].T.reshape(ROWS // 64, 2, 32, pw)
+        return 0
+
+    lax.fori_loop(0, nrb, turn, 0)
+
+    half_rows = ROWS // 32
+
+    def att_other(j, _):
+        at = pl.ds(j * half_rows, half_rows)
+        o = ob[at, oth].reshape(ROWS, pw)
+        sb1[at] = mm(NT, o, wop[...]).astype(BF).reshape(half_rows, 32, dim)
+        return 0
+
+    def att_own(j, _):
+        at = pl.ds(j * half_rows, half_rows)
+        o = ob[at, c].reshape(ROWS, pw)
+        own[at] = mm(NT, o, wop[...]).reshape(half_rows, 32, dim)
+        return 0
+
+    lax.fori_loop(0, groups // half_rows, att_other, 0)
+    swap_start(2, sb1, rb1)
+    lax.fori_loop(0, groups // half_rows, att_own, 0)
+    ag1(4)
+    wait(rb1, ex_r.at[2])
+
+    def norm_two(i, _):
+        att = own[i] + rb1[i].astype(F32)
+        x1 = xbuf[i].astype(F32) + jnp.where(live_at(i), att, 0.0)
+        x1b[i] = x1
+        r = lax.rsqrt(mean(x1 * x1) + EPS)
+        r2b[i] = jnp.broadcast_to(r, (32, 128))
+        bbuf[i, c] = (x1 * r).astype(BF)
+        return 0
+
+    lax.fori_loop(0, groups, norm_two, 0, unroll=2)
+    swap_start(3, bbuf.at[:, c], bbuf.at[:, c])
+    wait(dfb.at[:, oth], ex_r.at[1])
+    ag2(2)
+    wait(bbuf.at[:, oth], ex_r.at[3])
+
+    def ffn(f, _):
+        ag3(f)
+
+        def one(i, _):
+            b = bbuf[blk(i)].reshape(ROWS, dim)
+            d = dfb[blk(i)].reshape(ROWS, dim)
+            w_gu = w_f[f, :, :, :, :, 0 : 2 * chunk].reshape(dim, 2 * chunk)
+            w_d = w_f[f, :, :, :, :, 2 * chunk : 3 * chunk].reshape(dim, chunk)
+            gu = mm(NN, b, w_gu)
+            dh = mm(NN, d, w_d)
+            gate, up = gu[:, 0:chunk], gu[:, chunk:]
+            sg = jax.nn.sigmoid(gate)
+            silu = gate * sg
+            hid = (silu * up).astype(BF)
+            dgate = (dh * up * sg * (1.0 + gate * (1.0 - sg))).astype(BF)
+            dup = (dh * silu).astype(BF)
+            at = pl.ds(pl.multiple_of(i * ROWS, ROWS), ROWS)
+            act[at, 0:chunk] = dgate
+            act[at, chunk : 2 * chunk] = dup
+            act[at, 2 * chunk : 3 * chunk] = hid
+            facc[blk(i)] += mm(NT, hid, w_d).reshape(ROWS // 64, 2, 32, dim)
+            dgu = jnp.concatenate([dgate, dup], axis=1)
+            uacc[blk(i)] += mm(NT, dgu, w_gu).reshape(ROWS // 64, 2, 32, dim)
+            return 0
+
+        lax.fori_loop(0, nrb, one, 0)
+        ag_done(f)
+        for m in range(2):
+            feats = slice(m * half, (m + 1) * half)
+            zs = slice(m * nz // 2, (m + 1) * nz // 2)
+            left = bbuf[:, :, :, feats].reshape(seq_len, half)
+            t = mm(TN, left, act[:, 0 : 2 * chunk]).astype(BF)
+            w_f[f, zs, :, :, :, 0 : 2 * chunk] = t.reshape(nz // 2, 2, 2, nrow, 2 * chunk)
+            left = dfb[:, :, :, feats].reshape(seq_len, half)
+            t = mm(TN, left, act[:, 2 * chunk : 3 * chunk]).astype(BF)
+            w_f[f, zs, :, :, :, 2 * chunk : 3 * chunk] = t.reshape(nz // 2, 2, 2, nrow, chunk)
+        rs0(f)
+
+        @pl.when(f + 3 < nf)
+        def _():
+            ag2(f + 3)
+
+        @pl.when(f >= 1)
+        def _():
+            rs1(f - 1)
+
+        @pl.when(f >= 2)
+        def _():
+            rs2(f - 2)
+
+        return 0
+
+    lax.fori_loop(0, nf, ffn, 0)
+
+    wait(sb1, ex_s.at[2])
+
+    def cast_u(i, _):
+        sb1[i] = uacc[i, oth].astype(BF)
+        return 0
+
+    def cast_f(i, _):
+        sb2[i] = facc[i, oth].astype(BF)
+        return 0
+
+    lax.fori_loop(0, groups, cast_u, 0)
+    swap_start(4, sb1, rb1)
+    lax.fori_loop(0, groups, cast_f, 0)
+    swap_start(5, sb2, rb2)
+    rs1(nf - 1)
+
+    @pl.when(home)
+    def _():
+        wait(xs.at[pl.ds(0, groups - 1)], a2a_s)
+
+    @pl.when(away)
+    def _():
+        wait(xs, a2a_s)
+
+    wait(rb1, ex_r.at[4])
+    wait(rb2, ex_r.at[5])
+    wait(bbuf.at[:, c], ex_s.at[3])
+
+    def norm_three(i, _):
+        alive = live_at(i)
+        x1 = x1b[i]
+        r = r2b[i][:, 0:1]
+        n = x1 * r
+        u = uacc[i, c] + rb1[i].astype(F32)
+        dx1 = dybuf[i].astype(F32) + r * (u - n * mean(u * n))
+        bbuf[i, c] = jnp.where(alive, dx1, 0.0).astype(BF)
+        ffn_out = facc[i, c] + rb2[i].astype(F32)
+        xs[i] = (x1 + jnp.where(alive, ffn_out, 0.0)).astype(BF)
+        x1b[i] = dx1
+        return 0
+
+    lax.fori_loop(0, groups, norm_three, 0, unroll=2)
+    swap_start(6, bbuf.at[:, c], bbuf.at[:, c])
+
+    @pl.when(home)
+    def _():
+        pltpu.make_async_copy(xs, lo_ref, lo_r).start()
+
+    @pl.when(away)
+    def _():
+        rc(xs, lo_ref, lo_s, lo_r, swap).start()
+
+    rs2(nf - 2)
+
+    def turn_k(i, _):
+        at = pl.ds(pl.multiple_of(i * ROWS, ROWS), ROWS)
+        t = kb[blk(i)].reshape(ROWS, pw).T
+        for h in range(pw // 64):
+            for part in range(2):
+                first = (h // 4) * 256 + part * 128 + (h % 4) * 32
+                vt[h * 64 + part * 32 : h * 64 + part * 32 + 32, at] = t[first : first + 32]
+        return 0
+
+    lax.fori_loop(0, nrb, turn_k, 0)
+    facc[...] = jnp.zeros_like(facc)
+    uacc[...] = jnp.zeros_like(uacc)
+    heads16 = lax.broadcasted_iota(jnp.int32, (16, pw), 0)
+    pick = jnp.where(
+        (lax.broadcasted_iota(jnp.int32, (16, pw), 1) >> 6) == heads16, 1.0, 0.0
+    ).astype(BF)
+    wait(bbuf.at[:, oth], ex_r.at[6])
+
+    def out_back(i, _):
+        at = pl.ds(pl.multiple_of(i * ROWS, ROWS), ROWS)
+        t = mm(NN, bbuf[blk(i)].reshape(ROWS, dim), wop[...]).astype(BF)
+        dob[blk(i)] = t.reshape(ROWS // 64, 2, 32, pw)
+        prod = t.astype(F32) * ob[blk(i)].reshape(ROWS, pw).astype(F32)
+        delta[:, at] = mm(NT, pick, prod.astype(BF))
+        return 0
+
+    lax.fori_loop(0, nrb, out_back, 0)
+    ag_done("o")
+    for m in range(2):
+        left = bbuf[:, :, :, m * half : (m + 1) * half].reshape(seq_len, half)
+        t = mm(TN, left, ob[...].reshape(seq_len, pw)).astype(BF)
+        zs = slice(m * nz // 2, (m + 1) * nz // 2)
+        w_o[zs] = mm(NT, t, ev[...]).astype(BF).reshape(nz // 2, 2, 2, nrow, hw)
+    rs0("o")
+
+    def attend_back(i):
+        keys = (i + 1) * ROWS
+
+        def group(g, _):
+            lanes = pl.ds(pl.multiple_of(g * 256, 256), 256)
+            q = rows_of(qb, i * ROWS, ROWS, lanes)
+            d = rows_of(dob, i * ROWS, ROWS, lanes)
+            for hh in range(4):
+                qm = jnp.where(((lane >> 5) & 3) == hh, q, jnp.zeros_like(q))
+                dm = jnp.where((lane >> 6) == hh, d, jnp.zeros_like(d))
+                row_lse = lse[pl.ds(g * 4 + hh, 1), i * ROWS : keys]
+                row_delta = delta[pl.ds(g * 4 + hh, 1), i * ROWS : keys]
+
+                def part(first, count, masked):
+                    s = mm(NT, rows_of(kb, first, count, lanes), qm)
+                    if masked:
+                        s = jnp.where(diag, s, -1e30)
+                    p = jnp.exp2(s - row_lse)
+                    dp_ = mm(NT, rows_of(vb, first, count, lanes), dm)
+                    ds = (p * (dp_ - row_delta)).astype(BF)
+                    at = pl.ds(first // 64, count // 64)
+                    uacc[at, :, :, lanes] += mm(NN, p.astype(BF), dm).reshape(
+                        count // 64, 2, 32, 256
+                    )
+                    facc[at, :, :, lanes] += mm(NN, ds, qm).reshape(count // 64, 2, 32, 256)
+                    return ds
+
+                ds = part(i * ROWS, ROWS, True)
+                if i:
+                    ds = jnp.concatenate([part(0, i * ROWS, False), ds], axis=0)
+                hs = pl.multiple_of(g * 256 + hh * 64, 64)
+                t = mm(NN, vt[pl.ds(hs, 64), 0:keys], ds) * score_scale
+                c_now, s_now = ct[:, i * ROWS : keys], st[:, i * ROWS : keys]
+                f1, f2 = t[0:32], t[32:64]
+                hs = pl.multiple_of(g * 256 + hh * 32, 32)
+                ot[pl.ds(hs, 32), i * ROWS : keys] = (f1 * c_now + f2 * s_now).astype(BF)
+                ot[pl.ds(hs + 128, 32), i * ROWS : keys] = (f2 * c_now - f1 * s_now).astype(BF)
+            return 0
+
+        lax.fori_loop(0, pw // 256, group, 0)
+
+    with_steps(
+        attend_back,
+        ((0, lambda: rs2(nf - 1)), (1, lambda: rs1("o")), (2, lambda: rs2("o"))),
+    )
+
+    def turn_back(i, _):
+        at = pl.ds(pl.multiple_of(i * ROWS, ROWS), ROWS)
+        qb[blk(i)] = ot[:, at].T.reshape(ROWS // 64, 2, 32, pw)
+        vb[blk(i)] = uacc[blk(i), :, :, 0:pw].astype(BF)
+        cos, sin = cosb[at, :], sinb[at, :]
+        for g in range(pw // 256):
+            f1 = facc[blk(i), :, :, g * 256 : g * 256 + 128].reshape(ROWS, 128)
+            f2 = facc[blk(i), :, :, g * 256 + 128 : g * 256 + 256].reshape(ROWS, 128)
+            kb[blk(i), :, :, g * 256 : g * 256 + 128] = (
+                ((f1 * cos + f2 * sin) * (1.0 / LOG2E)).astype(BF).reshape(ROWS // 64, 2, 32, 128)
+            )
+            kb[blk(i), :, :, g * 256 + 128 : g * 256 + 256] = (
+                ((f2 * cos - f1 * sin) * (1.0 / LOG2E)).astype(BF).reshape(ROWS // 64, 2, 32, 128)
+            )
+        return 0
+
+    lax.fori_loop(0, nrb, turn_back, 0)
+    ag_done("a")
+    for t, (src, e) in enumerate(((qb, eqk), (kb, eqk), (vb, ev))):
+        for m in range(2):
+            left = abuf[:, :, :, m * half : (m + 1) * half].reshape(seq_len, half)
+            part = mm(TN, left, src[...].reshape(seq_len, pw)).astype(BF)
+            zs = slice(m * nz // 2, (m + 1) * nz // 2)
+            w_a[zs, :, :, :, t * hw : (t + 1) * hw] = (
+                mm(NT, part, e[...]).astype(BF).reshape(nz // 2, 2, 2, nrow, hw)
+            )
+    rs0("a")
+    wait(sb1, ex_s.at[4])
+
+    def da_rows(at, which):
+        total = None
+        for t, src in enumerate((qb, kb, vb)):
+            term = mm(NT, src[at, which].reshape(ROWS, pw), wp[:, t * pw : (t + 1) * pw])
+            total = term if total is None else total + term
+        return total.reshape(half_rows, 32, dim)
+
+    def da_other(j, _):
+        at = pl.ds(j * half_rows, half_rows)
+        sb1[at] = da_rows(at, oth).astype(BF)
+        return 0
+
+    def da_own(j, _):
+        at = pl.ds(j * half_rows, half_rows)
+        own[at] = da_rows(at, c)
+        return 0
+
+    lax.fori_loop(0, groups // half_rows, da_other, 0)
+    swap_start(7, sb1, rb1)
+    lax.fori_loop(0, groups // half_rows, da_own, 0)
+
+    @pl.when(away)
+    def _():
+        wait(xs, lo_s)
+
+    wait(lo_ref, lo_r)
+    wait(rb1, ex_r.at[7])
+
+    def norm_four(i, _):
+        rows_now = xbuf[i].astype(F32)
+        r = r1b[i][:, 0:1]
+        n = rows_now * r
+        u = own[i] + rb1[i].astype(F32)
+        dx = x1b[i] + r * (u - n * mean(u * n))
+        xs[i] = dx.astype(BF)
+        same = (i == dp) & (c == y)
+
+        @pl.when(same)
+        def _():
+            pltpu.make_async_copy(xs.at[i], ret.at[slot], ret_r).start()
+
+        @pl.when(jnp.logical_not(same))
+        def _():
+            rc(xs.at[i], ret.at[slot], ret_s, ret_r, (i, c)).start()
+
+        return 0
+
+    lax.fori_loop(0, groups, norm_four, 0)
+    rs1("a")
+
+    def finish_f(f, total):
+        sums = jnp.zeros((nrow, 1), F32) if total is None else total
+        t = rs3(f)
+        at = pl.ds(pl.multiple_of(f * chunk, chunk), chunk)
+        dg, du = t[:, 0:chunk], t[:, chunk : 2 * chunk]
+        dg_out[:, at] = dg * gain2
+        du_out[:, at] = du * gain2
+        dd_out[:, at] = t[:, 2 * chunk : 3 * chunk]
+        both = dg * wg[:, at].astype(F32) + du * wu[:, at].astype(F32)
+        return sums + jnp.sum(both, axis=1, keepdims=True)
+
+    sums2 = lax.fori_loop(0, nf, finish_f, jnp.zeros((nrow, 1), F32))
+    rs2("a")
+    do_out[...] = rs3("o")
+    t = rs3("a")
+    sums1 = jnp.zeros((nrow, 1), F32)
+    for i, (w, out) in enumerate(((wq, dq_out), (wk, dk_out), (wv, dv_out))):
+        part = t[:, i * hw : (i + 1) * hw]
+        out[...] = part * gain1
+        sums1 = sums1 + jnp.sum(part * w[...].astype(F32), axis=1, keepdims=True)
+    first_half = lax.broadcasted_iota(jnp.int32, (nrow, 128), 1) < 64
+    gs[...] = jnp.where(first_half, sums1, sums2)
+    rc(gs, gr, gg_s, gg_r, ynbr).start()
+
+    wait(ret, ret_r)
+
+    def restore(s, _):
+        def find(j, at):
+            return jnp.where(deal[j] == s, j, at)
+
+        gi_ref[s] = ret[lax.fori_loop(0, groups, find, 0)]
+        return 0
+
+    lax.fori_loop(0, groups, restore, 0)
+    wait(gr, gg_r)
+    dgain_out[...] = gs[...] + gr[...]
+
+    wait(gs, gg_s)
+    for f in range(nf):
+        rs_done(f)
+    rs_done("o")
+    rs_done("a")
+
+    @pl.when(away)
+    def _():
+        wait(dybuf, dy_s)
+
+    @pl.when(home)
+    def _():
+        wait(xs.at[pl.ds(0, groups - 1)], ret_s)
+
+    @pl.when(away)
+    def _():
+        wait(xs, ret_s)
+
+    wait(abuf.at[:, c], ex_s.at[0])
+    wait(dfb.at[:, c], ex_s.at[1])
+    wait(sb2, ex_s.at[5])
+    wait(bbuf.at[:, c], ex_s.at[6])
+    wait(sb1, ex_s.at[7])
+
+
+def rotary_tables(count):
+    lanes = np.arange(128) % 32
+    frequency = np.where(lanes < HD // 2, BASE ** (-2.0 * lanes / HD), 0.0)
+    high = np.zeros((32, 128))
+    high[:count] = 32.0 * np.arange(count)[:, None] * frequency[None, :]
+    low = np.arange(32)[:, None] * frequency[None, :]
+    return np.stack([np.cos(high), np.sin(high), np.cos(low), np.sin(low)]).astype(np.float32)
+
+
+def fused_body(
+    x_given, dealing, seq_lengths, first_gain, query_weight, key_weight, value_weight,
+    output_weight, second_gain, gate_weight, up_weight, down_weight, grad_output,
+):
+    groups, piece_rows, dim = x_given.shape
+    hw = query_weight.shape[1]
+    local_hidden = gate_weight.shape[1]
+    chunk = 256
+    nf = local_hidden // chunk
+    nz = groups // 4
+    rows = query_weight.shape[0]
+    pw = hw // HD * 64
+    seq_len = groups * 64
+    vm, anym, sm = (
+        pl.BlockSpec(memory_space=pltpu.VMEM),
+        pl.BlockSpec(memory_space=pl.ANY),
+        pl.BlockSpec(memory_space=pltpu.SMEM),
+    )
+    blocks = (groups, piece_rows, dim)
+    pairs = (groups, 2, piece_rows)
+
+    def gathered(width, lead=()):
+        return pltpu.VMEM(lead + (nz, 2, 2, rows, width), BF)
+
+    kd = nz // 2
+
+    def landing(width, lead=()):
+        return [
+            pltpu.VMEM(lead + (nz, 2, rows, width), BF),
+            pltpu.VMEM(lead + (kd, 2, 2, rows, width), BF),
+            pltpu.VMEM(lead + (nz - kd, 2, rows, width), BF),
+            pltpu.VMEM(lead + (nz, rows, width), BF),
+        ]
+
+    units = nf + 2
+    dma = pltpu.SemaphoreType.DMA
+    scratch = (
+        [pltpu.VMEM(blocks, BF)] * 3
+        + [pltpu.VMEM((rows, 3 * hw), BF), pltpu.VMEM((nf, rows, 3 * chunk), BF)]
+        + [gathered(3 * hw), gathered(hw), gathered(3 * chunk, (nf,))]
+        + [pltpu.VMEM((dim, 3 * pw), BF), pltpu.VMEM((dim, pw), BF)]
+        + [pltpu.VMEM((hw, pw), BF)] * 2
+        + [pltpu.VMEM((seq_len, 128), F32)] * 2
+        + [pltpu.VMEM((32, seq_len), F32)] * 2
+        + [pltpu.VMEM(pairs + (dim,), BF)]
+        + [pltpu.VMEM(pairs + (pw,), BF)] * 3
+        + [pltpu.VMEM((pw, seq_len), BF)] * 2
+        + [pltpu.VMEM(pairs + (pw,), BF)]
+        + [pltpu.VMEM((8, seq_len), F32)]
+        + [pltpu.VMEM(blocks, F32)]
+        + [pltpu.VMEM(blocks, BF)] * 4
+        + [pltpu.VMEM(blocks, F32)]
+        + [pltpu.VMEM((groups, piece_rows, 128), F32)] * 2
+        + [pltpu.VMEM(pairs + (dim,), BF)] * 2
+        + [pltpu.VMEM(pairs + (dim,), F32)] * 2
+        + [pltpu.VMEM((seq_len, 3 * chunk), BF)]
+        + [pltpu.VMEM(pairs + (pw,), BF)]
+        + [pltpu.VMEM((16, seq_len), F32)]
+        + landing(3 * hw)
+        + landing(hw)
+        + landing(3 * chunk, (nf,))
+        + [pltpu.VMEM(blocks, BF)]
+        + [pltpu.VMEM((rows, 128), F32)] * 3
+        + [dma(())] * 4
+        + [dma((units,)), dma((units,)), dma((units,)), dma((units, 2)), dma((units, nz + 3))]
+        + [dma((units, 2)), dma((units, 2)), dma((units,)), dma((units, 2 * nz + 2))]
+        + [dma((8,)), dma((8,))]
+        + [dma(())] * 6
+    )
+    small = jax.ShapeDtypeStruct((rows, hw), F32)
+    wide = jax.ShapeDtypeStruct((rows, local_hidden), F32)
+    piece = jax.ShapeDtypeStruct(blocks, BF)
+    outs = pl.pallas_call(
+        functools.partial(fused_kernel, (nz, nf, dim, hw, chunk, rows)),
+        out_shape=[piece, piece, small, small, small, small, wide, wide, wide]
+        + [jax.ShapeDtypeStruct((rows, 128), F32)],
+        in_specs=[sm, sm, vm, anym] + [vm] * 10,
+        out_specs=[anym] + [vm] * 9,
+        scratch_shapes=scratch,
+        compiler_params=pltpu.CompilerParams(
+            collective_id=0, has_side_effects=True, vmem_limit_bytes=VMEM_LIMIT
+        ),
+        name="layer",
+    )(
+        dealing, seq_lengths, x_given, grad_output.reshape(blocks),
+        first_gain.astype(F32).reshape(rows, 1), second_gain.astype(F32).reshape(rows, 1),
+        query_weight, key_weight, value_weight, output_weight, gate_weight, up_weight, down_weight,
+        rotary_tables(seq_len // 32),
+    )
+    layer_out, grad_in, gq, gk, gv, go, gg, gu, gd, gains = outs
+    return (
+        layer_out.reshape(grad_output.shape), grad_in, gains[:, 0], gq, gk, gv, go,
+        gains[:, 64], gg, gu, gd,
+    )
+
+
+def fits_fused(mesh):
+    return mesh.shape["tensor"] == 2 and mesh.shape["dp"] % 8 == 0
+
+
 def solution(mesh):
     placed = (
         P(None, ("dp", "tensor"), None),
@@ -443,7 +1381,7 @@
         P("dp", None, "tensor", None, None),
     )
     return jax.shard_map(
-        body,
+        fused_body if fits_fused(mesh) else body,
         mesh=mesh,
         in_specs=placed,
         out_specs=(

time: 1070 us -> 239 us (0.22)
  waiting for transfers between devices: 657 us -> 0 us
  Pallas kernels: 0 us -> 226 us
  blocking collectives: 141 us -> 0 us
  matrix products: 114 us -> 0 us
  local copies, waits for them, and re-layouts: 62.3 us -> 11.3 us
  other arithmetic: 49.6 us -> 0.66 us
  between operations: 20.7 us -> 0.67 us
  starting transfers between devices: 14.8 us -> 0 us
    reduce_scatter x12 -> x0, waiting for transfers between devices: 469 us -> none  [the longest x1 73.5 us: body(): lax.psum_scatter(down_term.astype(jnp.bfloat16), 'dp', scatter_dimension=...]
    pallas_call x0 -> x1, Pallas kernels: none -> 226 us  [fused_body(): pl.pallas_call(functools.partial(fused_kernel, (nz, nf, dim, hw, chunk, r...]
    all_gather x5 -> x0, waiting for transfers between devices: 136 us -> none  [the longest x1 43.5 us: body(): lax.all_gather(columns[1], 'dp', axis=0, tiled=True)]
    dot_general x36 -> x0, matrix products: 114 us -> none  [the longest x5 30 us: row_dot(): return jnp.dot(left_side, right_side, preferred_element_type=jnp.float32)]
    all_gather x7 -> x0, blocking collectives: 105 us -> none  [the longest x1 23.1 us: body(): lax.all_gather(query_weight, 'dp', axis=0, tiled=True)]
    unnamed x19 -> x0, waiting for transfers between devices: 52.1 us -> none
    unnamed x2 -> x0, blocking collectives: 35.2 us -> none
    convert_element_type x19 -> x0, other arithmetic: 26.6 us -> none  [the longest x4 5.62 us: body(): summed = (lax.psum_scatter(gain_pair.astype(jnp.bfloat16), 'dp', scatter_...]
  transfers between devices with their start and end apart: 20 -> 0, of which waited for: 16 -> 0; matrix products, arithmetic and copies ran while one was open for 6% -> 0% of each run, Pallas kernels for 0% -> 0%
where the time goes in v1:
time: 239 us
  Pallas kernels  226 us (95%)
  local copies, waits for them, and re-layouts  11.3 us (5%)
    pallas_call x1, Pallas kernels, fused_body(): pl.pallas_call(functools.partial(fused_kernel, (nz, nf, dim, hw, chunk, r...  226 us
    unnamed x27, local copies, waits for them, and re-layouts  8.35 us

profile of v1, /device:TPU:25, one launch (start us, length us, event | category | flops | bytes accessed | tf_op | source)
XLA Modules:
  0.0 238.9 jit_solution(7756617985390539539)
XLA Ops:
  0.6 0.7 bitcast_convert_fusion.1
  1.3 0.0 copy-start.8
  1.3 0.7 copy.28.g1
  2.0 0.0 copy-done.8
  2.0 0.7 copy.29.g2
  2.7 226.3 %layer.1 = (bf16[16,32,768]{2,1,0:T(8,128)(2,1)}, bf16[16,32,768]{2,1,0:T(8,128)(2,1)}, f32[48,384]{1,0:T(8,128)}, f32[48,384]{1,0:T(8,128)}, f32[48,384]{1,0:T(...) custom-call(s32[16]{0:T(128)} %deal.1, s32[16]{0:T(128)} %lens.1, ...), custom_call_target="tpu_custom_call" | custom-call | tf_op jit(solution)/shard_map/layer/pallas_call | solution.py:1339
  229.1 1.5 slice_reduce_fusion
  230.6 2.1 copy.40
  232.7 0.0 copy-done
  232.7 0.9 copy.41
  233.6 0.0 copy-done.7
  233.6 0.6 copy.42
  234.3 0.0 copy-done.6
  234.3 0.6 copy.43
  234.9 0.0 copy-done.5
  234.9 0.6 copy.44
  235.5 0.0 copy-done.4
  235.5 0.6 copy.45
  236.2 0.0 copy-done.3
  236.2 0.7 copy.46
  236.9 0.3 copy-done.2
  237.2 0.7 copy.47
  237.9 0.3 copy-done.1
  238.2 0.7 copy.48
  (9 shorter events, 0.0 us)
Async XLA Ops:
  1.3 0.7 copy-start.8
  230.6 2.1 copy-start
  232.7 0.9 copy-start.7
  232.7 1.5 copy-start.6
  233.6 1.3 copy-start.5
  233.6 1.9 copy-start.4
  234.3 1.9 copy-start.3
  236.2 1.0 copy-start.2
  237.2 1.0 copy-start.1

commit v2 on v1

--- a/solution.py
+++ b/solution.py
@@ -449,7 +449,7 @@
 def fused_kernel(
     shape,
     deal, lens, x_ref, dy_ref, g1, g2, wq, wk, wv, wo, wg, wu, wd, tab,
-    lo_ref, gi_ref, dq_out, dk_out, dv_out, do_out, dg_out, du_out, dd_out, dgain_out,
+    lo_ref, gi_ref, dq_out, dk_out, dv_out, do_out, dg_out, du_out, dd_out, dg1_out, dg2_out,
     xs, xbuf, dybuf, src_a, src_f, w_a, w_o, w_f, wp, wop, eqk, ev, cosb, sinb, ct, st,
     abuf, qb, kb, vb, vt, ot, ob, lse, own, sb1, sb2, rb1, rb2, x1b, r1b, r2b, bbuf, dfb,
     facc, uacc, act, dob, delta, rx_a, ry_a, ry2_a, rz_a, rx_o, ry_o, ry2_o, rz_o,
@@ -463,6 +463,7 @@
     half = dim // 2
     nrb = seq_len // ROWS
     kd = nz // 2
+    kg = nz // 2
     dp = lax.axis_index("dp")
     y = lax.axis_index("tensor")
     z = dp // 4
@@ -501,30 +502,6 @@
     lax.fori_loop(1, ndev, greet, 0)
     pl.semaphore_wait(bar, ndev - 1)
 
-    def stage(j, _):
-        xs[j] = x_ref[deal[j]]
-        return 0
-
-    lax.fori_loop(0, groups, stage, 0)
-
-    def deal_out(i, _):
-        j = lax.rem(slot + i, groups)
-        dpd = (j // 2) * 2 + y
-        td = j % 2
-        same = (dpd == dp) & (td == y)
-
-        @pl.when(same)
-        def _():
-            pltpu.make_async_copy(xs.at[j], xbuf.at[dp], a2a_r).start()
-
-        @pl.when(jnp.logical_not(same))
-        def _():
-            rc(xs.at[j], xbuf.at[dp], a2a_s, a2a_r, (dpd, td)).start()
-
-        return 0
-
-    lax.fori_loop(0, groups, deal_out, 0)
-
     def unit(k):
         if isinstance(k, str):
             return (src_a, w_a, 0) if k == "a" else (wo, w_o, 1)
@@ -559,13 +536,13 @@
         @pl.when(home)
         def _():
             wait(buf.at[:, xb], ag_x.at[n])
-            part = buf.at[pl.ds(0, kd), xb]
+            part = buf.at[pl.ds(0, kg), xb]
             rc(part, part, ag_s.at[n, nz + 2], ag_d.at[n, 0], ynbr).start()
 
         @pl.when(away)
         def _():
             wait(buf.at[:, x], ag_y.at[n])
-            part = buf.at[pl.ds(kd, nz - kd), x]
+            part = buf.at[pl.ds(kg, nz - kg), x]
             rc(part, part, ag_s.at[n, nz + 2], ag_d.at[n, 1], xnbr).start()
 
     def ag3(k):
@@ -573,8 +550,8 @@
 
         @pl.when(away)
         def _():
-            wait(buf.at[pl.ds(0, kd), xb], ag_d.at[n, 0])
-            wait(buf.at[pl.ds(kd, nz - kd), xb], ag_d.at[n, 1])
+            wait(buf.at[pl.ds(0, kg), xb], ag_d.at[n, 0])
+            wait(buf.at[pl.ds(kg, nz - kg), xb], ag_d.at[n, 1])
 
     def ag_done(k):
         src, buf, n = unit(k)
@@ -585,12 +562,12 @@
         def _():
             wait(buf.at[:, x], ag_s.at[n, nz])
             wait(buf.at[:, x], ag_s.at[n, nz + 1])
-            wait(buf.at[pl.ds(0, kd), xb], ag_s.at[n, nz + 2])
+            wait(buf.at[pl.ds(0, kg), xb], ag_s.at[n, nz + 2])
 
         @pl.when(away)
         def _():
             wait(src, ag_s.at[n, nz - 1])
-            wait(buf.at[pl.ds(kd, nz - kd), x], ag_s.at[n, nz + 2])
+            wait(buf.at[pl.ds(kg, nz - kg), x], ag_s.at[n, nz + 2])
 
     def rs_unit(k):
         if isinstance(k, str):
@@ -709,20 +686,44 @@
             total = part if total is None else total + part
         return total
 
-    gain1 = g1[...]
-    gain2 = g2[...]
+    square = (nrow, nrow)
+    on_diag = lax.broadcasted_iota(jnp.int32, square, 0) == lax.broadcasted_iota(
+        jnp.int32, square, 1
+    )
+
+    def column(ref):
+        spread = jnp.where(on_diag, ref[...].astype(F32), 0.0)
+        return jnp.sum(spread, axis=1, keepdims=True)
+
+    gain1 = column(g1)
+    gain2 = column(g2)
     for i, w in enumerate((wq, wk, wv)):
         src_a[:, i * hw : (i + 1) * hw] = (w[...].astype(F32) * gain1).astype(BF)
     zsend("a")
-    zsend("o")
-
-    @pl.when(home)
-    def _():
-        pltpu.make_async_copy(dy_ref, dybuf, dy_r).start()
-
-    @pl.when(away)
-    def _():
-        rc(dy_ref, dybuf, dy_s, dy_r, swap).start()
+
+    def stage(j, _):
+        xs[j] = x_ref[deal[j]]
+        return 0
+
+    lax.fori_loop(0, groups, stage, 0)
+
+    def deal_out(i, _):
+        j = lax.rem(slot + i, groups)
+        dpd = (j // 2) * 2 + y
+        td = j % 2
+        same = (dpd == dp) & (td == y)
+
+        @pl.when(same)
+        def _():
+            pltpu.make_async_copy(xs.at[j], xbuf.at[dp], a2a_r).start()
+
+        @pl.when(jnp.logical_not(same))
+        def _():
+            rc(xs.at[j], xbuf.at[dp], a2a_s, a2a_r, (dpd, td)).start()
+
+        return 0
+
+    lax.fori_loop(0, groups, deal_out, 0)
 
     for f in range(nf):
         cols = slice(f * chunk, (f + 1) * chunk)
@@ -751,8 +752,6 @@
     eqk[...] = jnp.where((row == spot) & (low < HD // 2), 1.0, 0.0).astype(BF)
     low = col & 63
     ev[...] = jnp.where((row == (col >> 6) * HD + low) & (low < HD), 1.0, 0.0).astype(BF)
-    facc[...] = jnp.zeros_like(facc)
-    uacc[...] = jnp.zeros_like(uacc)
 
     length = lens[deal[slot]]
 
@@ -770,25 +769,31 @@
         return pl.ds(i * (ROWS // 64), ROWS // 64)
 
     ag1("a")
-    ag1("o")
+    zsend("o")
     zsend(0)
-    zsend(1)
+
+    @pl.when(home)
+    def _():
+        pltpu.make_async_copy(dy_ref, dybuf, dy_r).start()
+
+    @pl.when(away)
+    def _():
+        rc(dy_ref, dybuf, dy_s, dy_r, swap).start()
+
+    ag2("a")
     wait(xbuf, a2a_r)
-    wait(dybuf, dy_r)
 
     def norm_one(i, _):
         rows_now = xbuf[i].astype(F32)
         r = lax.rsqrt(mean(rows_now * rows_now) + EPS)
         r1b[i] = jnp.broadcast_to(r, (32, 128))
         abuf[i, c] = (rows_now * r).astype(BF)
-        dfb[i, c] = jnp.where(live_at(i), dybuf[i], jnp.zeros((32, dim), BF))
         return 0
 
     lax.fori_loop(0, groups, norm_one, 0, unroll=2)
     swap_start(0, abuf.at[:, c], abuf.at[:, c])
-    swap_start(1, dfb.at[:, c], dfb.at[:, c])
-    ag2("a")
-    ag1(0)
+    ag1("o")
+    zsend(1)
     ag3("a")
     for i in range(3):
         e = eqk if i < 2 else ev
@@ -822,9 +827,9 @@
         return 0
 
     lax.fori_loop(0, nrb, project, 0)
+    ag1(0)
+    ag2("o")
     zsend(2)
-    ag1(1)
-    ag2("o")
 
     lane = lax.broadcasted_iota(jnp.int32, (ROWS, 256), 1)
     diag = lax.broadcasted_iota(jnp.int32, (ROWS, ROWS), 0) <= lax.broadcasted_iota(
@@ -862,17 +867,24 @@
 
         lax.fori_loop(0, pw // 256, group, 0)
 
+    def during_zero():
+        ag1(1)
+        zsend(3)
+        ag3("o")
+        wop[...] = mm(NN, w_o[...].reshape(dim, hw), ev[...]).astype(BF)
+
     def during_one():
         ag2(0)
-        ag3("o")
-        wop[...] = mm(NN, w_o[...].reshape(dim, hw), ev[...]).astype(BF)
         ag1(2)
-        zsend(3)
         zsend(4)
 
     def during_two():
         ag2(1)
         ag1(3)
+
+    def mask_dy(i, _):
+        dfb[i, c] = jnp.where(live_at(i), dybuf[i], jnp.zeros((32, dim), BF))
+        return 0
 
     def with_steps(part, steps):
         for i in range(nrb):
@@ -881,7 +893,10 @@
                 if min(at, nrb - 1) == i:
                     step()
 
-    with_steps(attend, ((1, during_one), (2, during_two)))
+    with_steps(attend, ((0, during_zero), (1, during_one), (2, during_two)))
+    wait(dybuf, dy_r)
+    lax.fori_loop(0, groups, mask_dy, 0, unroll=2)
+    swap_start(1, dfb.at[:, c], dfb.at[:, c])
 
     def turn(i, _):
         at = pl.ds(pl.multiple_of(i * ROWS, ROWS), ROWS)
@@ -922,7 +937,6 @@
     lax.fori_loop(0, groups, norm_two, 0, unroll=2)
     swap_start(3, bbuf.at[:, c], bbuf.at[:, c])
     wait(dfb.at[:, oth], ex_r.at[1])
-    ag2(2)
     wait(bbuf.at[:, oth], ex_r.at[3])
 
     def ffn(f, _):
@@ -945,9 +959,20 @@
             act[at, 0:chunk] = dgate
             act[at, chunk : 2 * chunk] = dup
             act[at, 2 * chunk : 3 * chunk] = hid
-            facc[blk(i)] += mm(NT, hid, w_d).reshape(ROWS // 64, 2, 32, dim)
+            fpart = mm(NT, hid, w_d).reshape(ROWS // 64, 2, 32, dim)
             dgu = jnp.concatenate([dgate, dup], axis=1)
-            uacc[blk(i)] += mm(NT, dgu, w_gu).reshape(ROWS // 64, 2, 32, dim)
+            upart = mm(NT, dgu, w_gu).reshape(ROWS // 64, 2, 32, dim)
+
+            @pl.when(f == 0)
+            def _():
+                facc[blk(i)] = fpart
+                uacc[blk(i)] = upart
+
+            @pl.when(f > 0)
+            def _():
+                facc[blk(i)] += fpart
+                uacc[blk(i)] += upart
+
             return 0
 
         lax.fori_loop(0, nrb, one, 0)
@@ -963,9 +988,9 @@
             w_f[f, zs, :, :, :, 2 * chunk : 3 * chunk] = t.reshape(nz // 2, 2, 2, nrow, chunk)
         rs0(f)
 
-        @pl.when(f + 3 < nf)
-        def _():
-            ag2(f + 3)
+        @pl.when(f + 2 < nf)
+        def _():
+            ag2(f + 2)
 
         @pl.when(f >= 1)
         def _():
@@ -1043,8 +1068,6 @@
         return 0
 
     lax.fori_loop(0, nrb, turn_k, 0)
-    facc[...] = jnp.zeros_like(facc)
-    uacc[...] = jnp.zeros_like(uacc)
     heads16 = lax.broadcasted_iota(jnp.int32, (16, pw), 0)
     pick = jnp.where(
         (lax.broadcasted_iota(jnp.int32, (16, pw), 1) >> 6) == heads16, 1.0, 0.0
@@ -1089,10 +1112,14 @@
                     dp_ = mm(NT, rows_of(vb, first, count, lanes), dm)
                     ds = (p * (dp_ - row_delta)).astype(BF)
                     at = pl.ds(first // 64, count // 64)
-                    uacc[at, :, :, lanes] += mm(NN, p.astype(BF), dm).reshape(
-                        count // 64, 2, 32, 256
-                    )
-                    facc[at, :, :, lanes] += mm(NN, ds, qm).reshape(count // 64, 2, 32, 256)
+                    dv_part = mm(NN, p.astype(BF), dm).reshape(count // 64, 2, 32, 256)
+                    dk_part = mm(NN, ds, qm).reshape(count // 64, 2, 32, 256)
+                    if masked and hh == 0:
+                        uacc[at, :, :, lanes] = dv_part
+                        facc[at, :, :, lanes] = dk_part
+                    else:
+                        uacc[at, :, :, lanes] += dv_part
+                        facc[at, :, :, lanes] += dk_part
                     return ds
 
                 ds = part(i * ROWS, ROWS, True)
@@ -1228,7 +1255,9 @@
 
     lax.fori_loop(0, groups, restore, 0)
     wait(gr, gg_r)
-    dgain_out[...] = gs[...] + gr[...]
+    both = gs[...] + gr[...]
+    dg1_out[...] = jnp.sum(jnp.where(on_diag, both[:, 0:1], 0.0), axis=0, keepdims=True)
+    dg2_out[...] = jnp.sum(jnp.where(on_diag, both[:, 64:65], 0.0), axis=0, keepdims=True)
 
     wait(gs, gg_s)
     for f in range(nf):
@@ -1339,9 +1368,9 @@
     outs = pl.pallas_call(
         functools.partial(fused_kernel, (nz, nf, dim, hw, chunk, rows)),
         out_shape=[piece, piece, small, small, small, small, wide, wide, wide]
-        + [jax.ShapeDtypeStruct((rows, 128), F32)],
+        + [jax.ShapeDtypeStruct((1, rows), F32)] * 2,
         in_specs=[sm, sm, vm, anym] + [vm] * 10,
-        out_specs=[anym] + [vm] * 9,
+        out_specs=[anym] + [vm] * 10,
         scratch_shapes=scratch,
         compiler_params=pltpu.CompilerParams(
             collective_id=0, has_side_effects=True, vmem_limit_bytes=VMEM_LIMIT
@@ -1349,15 +1378,28 @@
         name="layer",
     )(
         dealing, seq_lengths, x_given, grad_output.reshape(blocks),
-        first_gain.astype(F32).reshape(rows, 1), second_gain.astype(F32).reshape(rows, 1),
+        first_gain.reshape(1, rows), second_gain.reshape(1, rows),
         query_weight, key_weight, value_weight, output_weight, gate_weight, up_weight, down_weight,
         rotary_tables(seq_len // 32),
     )
-    layer_out, grad_in, gq, gk, gv, go, gg, gu, gd, gains = outs
+    outs = pl.pallas_call(
+        pass_on,
+        out_shape=[jax.ShapeDtypeStruct(o.shape, o.dtype) for o in outs],
+        in_specs=[vm] * len(outs),
+        out_specs=[vm] * len(outs),
+        name="results",
+    )(*outs)
+    layer_out, grad_in, gq, gk, gv, go, gg, gu, gd, gain_one, gain_two = outs
     return (
-        layer_out.reshape(grad_output.shape), grad_in, gains[:, 0], gq, gk, gv, go,
-        gains[:, 64], gg, gu, gd,
-    )
+        layer_out.reshape(grad_output.shape), grad_in, gain_one.reshape(rows), gq, gk, gv, go,
+        gain_two.reshape(rows), gg, gu, gd,
+    )
+
+
+def pass_on(*refs):
+    count = len(refs) // 2
+    for i in range(count):
+        refs[count + i][...] = refs[i][...]
 
 
 def fits_fused(mesh):

time: 239 us -> 219 us (0.916)
  local copies, waits for them, and re-layouts: 11.3 us -> 0 us
  Pallas kernels: 226 us -> 218 us
    pallas_call x1, Pallas kernels: 226 us -> 215 us  [fused_body(): pl.pallas_call(functools.partial(fused_kernel, (nz, nf, dim, hw, chunk, r...]
    unnamed x27 -> x0, local copies, waits for them, and re-layouts: 8.35 us -> none
    pallas_call x0 -> x1, Pallas kernels: none -> 3.21 us  [fused_body(): pl.pallas_call(pass_on, out_shape=[jax.ShapeDtypeStruct(o.shape, o.dtype)...]
where the time goes in v2:
time: 219 us
  Pallas kernels  218 us (100%)
    pallas_call x1, Pallas kernels, fused_body(): pl.pallas_call(functools.partial(fused_kernel, (nz, nf, dim, hw, chunk, r...  215 us

profile of v2, /device:TPU:25, one launch (start us, length us, event | category | flops | bytes accessed | tf_op | source)
XLA Modules:
  0.0 218.8 jit_solution(7838216314900878979)
XLA Ops:
  0.6 214.9 %layer.1 = (bf16[16,32,768]{2,1,0:T(8,128)(2,1)}, bf16[16,32,768]{2,1,0:T(8,128)(2,1)}, f32[48,384]{1,0:T(8,128)}, f32[48,384]{1,0:T(8,128)}, f32[48,384]{1,0:T(...) custom-call(s32[16]{0:T(128)} %deal.1, s32[16]{0:T(128)} %lens.1, ...), custom_call_target="tpu_custom_call" | custom-call | tf_op jit(solution)/shard_map/layer/pallas_call | solution.py:1368
  215.5 3.2 %results.1 = (bf16[16,32,768]{2,1,0:T(8,128)(2,1)}, bf16[16,32,768]{2,1,0:T(8,128)(2,1)}, f32[48,384]{1,0:T(8,128)}, f32[48,384]{1,0:T(8,128)}, f32[48,384]{1,0:...) custom-call(bf16[16,32,768]{2,1,0:T(8,128)(2,1)} %get-tuple-element., ...), custom_call_target="tpu_custom_call" | custom-call | tf_op jit(solution)/shard_map/results/pallas_call | solution.py:1385

commit v3 on v2

--- a/solution.py
+++ b/solution.py
@@ -450,20 +450,20 @@
     shape,
     deal, lens, x_ref, dy_ref, g1, g2, wq, wk, wv, wo, wg, wu, wd, tab,
     lo_ref, gi_ref, dq_out, dk_out, dv_out, do_out, dg_out, du_out, dd_out, dg1_out, dg2_out,
-    xs, xbuf, dybuf, src_a, src_f, w_a, w_o, w_f, wp, wop, eqk, ev, cosb, sinb, ct, st,
-    abuf, qb, kb, vb, vt, ot, ob, lse, own, sb1, sb2, rb1, rb2, x1b, r1b, r2b, bbuf, dfb,
-    facc, uacc, act, dob, delta, rx_a, ry_a, ry2_a, rz_a, rx_o, ry_o, ry2_o, rz_o,
-    rx_f, ry_f, ry2_f, rz_f, ret, gs, gr, rsum,
+    xs, xbuf, dybuf, src_a, src_f, w_a, w_f, wp, wop, eqk, ev, cosb, sinb, ct, st,
+    abuf, qb, kb, vb, vt, ot, ob, lse, own, sb1, sb2, rb1, rb2, x1b, rb, bb0, bb1, dd0, dd1,
+    facc, uacc, act, delta, urecv, frecv, usend, fsend,
+    rx_a, ry_a, ry2_a, rz_a, rx_f, rz_f, ret, gs, gr,
     a2a_s, a2a_r, dy_s, dy_r, ag_z, ag_x, ag_y, ag_d, ag_s, rs_x, rs_y, rs_z, rs_s,
-    ex_s, ex_r, lo_s, lo_r, ret_s, ret_r, gg_s, gg_r,
+    agf_z, agf_f, agf_x, agf_s, rsf_x, rsf_z, rsf_s, ex_s, ex_r, b_s, b_r, us_s, us_r, fs_s, fs_r,
+    uy_s, uy_r, lo_r, ret_s, ret_r, gg_s, gg_r, free,
 ):
-    nz, nf, dim, hw, chunk, nrow = shape
+    nz, dim, hw, fq, nrow = shape
     groups = 4 * nz
     seq_len = 64 * groups
     half = dim // 2
     nrb = seq_len // ROWS
     kd = nz // 2
-    kg = nz // 2
     dp = lax.axis_index("dp")
     y = lax.axis_index("tensor")
     z = dp // 4
@@ -481,7 +481,7 @@
     partner = dev(z, x, oth, y)
     xnbr = dev(z, xb, c, y)
     ynbr = dev(z, x, c, yb)
-    swap = dev(z, x, oth, yb)
+    other_slot = (z * 2 + x) * 2 + yb
 
     def rc(src, dst, ss, rs, to):
         return pltpu.make_async_remote_copy(
@@ -503,9 +503,7 @@
     pl.semaphore_wait(bar, ndev - 1)
 
     def unit(k):
-        if isinstance(k, str):
-            return (src_a, w_a, 0) if k == "a" else (wo, w_o, 1)
-        return (src_f.at[k], w_f.at[k], k + 2)
+        return (wo if k == 3 else src_a.at[k]), w_a.at[k], k
 
     def zsend(k):
         src, buf, n = unit(k)
@@ -536,13 +534,13 @@
         @pl.when(home)
         def _():
             wait(buf.at[:, xb], ag_x.at[n])
-            part = buf.at[pl.ds(0, kg), xb]
+            part = buf.at[pl.ds(0, kd), xb]
             rc(part, part, ag_s.at[n, nz + 2], ag_d.at[n, 0], ynbr).start()
 
         @pl.when(away)
         def _():
             wait(buf.at[:, x], ag_y.at[n])
-            part = buf.at[pl.ds(kg, nz - kg), x]
+            part = buf.at[pl.ds(kd, nz - kd), x]
             rc(part, part, ag_s.at[n, nz + 2], ag_d.at[n, 1], xnbr).start()
 
     def ag3(k):
@@ -550,8 +548,8 @@
 
         @pl.when(away)
         def _():
-            wait(buf.at[pl.ds(0, kg), xb], ag_d.at[n, 0])
-            wait(buf.at[pl.ds(kg, nz - kg), xb], ag_d.at[n, 1])
+            wait(buf.at[pl.ds(0, kd), xb], ag_d.at[n, 0])
+            wait(buf.at[pl.ds(kd, nz - kd), xb], ag_d.at[n, 1])
 
     def ag_done(k):
         src, buf, n = unit(k)
@@ -562,35 +560,121 @@
         def _():
             wait(buf.at[:, x], ag_s.at[n, nz])
             wait(buf.at[:, x], ag_s.at[n, nz + 1])
-            wait(buf.at[pl.ds(0, kg), xb], ag_s.at[n, nz + 2])
+            wait(buf.at[pl.ds(0, kd), xb], ag_s.at[n, nz + 2])
 
         @pl.when(away)
         def _():
             wait(src, ag_s.at[n, nz - 1])
-            wait(buf.at[pl.ds(kg, nz - kg), x], ag_s.at[n, nz + 2])
+            wait(buf.at[pl.ds(kd, nz - kd), x], ag_s.at[n, nz + 2])
 
     def rs_unit(k):
-        if isinstance(k, str):
-            if k == "a":
-                return (w_a, rx_a, ry_a, ry2_a, rz_a, 0)
-            return (w_o, rx_o, ry_o, ry2_o, rz_o, 1)
-        return (w_f.at[k], rx_f.at[k], ry_f.at[k], ry2_f.at[k], rz_f.at[k], k + 2)
+        return w_a.at[k], rx_a.at[k], ry_a.at[k], ry2_a.at[k], rz_a.at[k], k
+
+    def src_unit(m, cc):
+        ref = wd if m == 2 else src_f.at[m]
+        return ref.at[:, cc * fq : (cc + 1) * fq]
+
+    at_end = (z == 0) | (z == nz - 1)
+    relay = jnp.where(z < nz // 2, nz - 1, 0)
+
+    def zsendf(m):
+        land = w_f.at[m, z, x, c]
+        for i in range(nz):
+            zt = lax.rem(z + i, nz)
+            span = jnp.abs(zt - z)
+            for cc in range(2):
+                src = src_unit(m, cc)
+                to = dev(zt, x, cc, y)
+                far = rc(src, land, agf_s.at[m, 2 * i + cc], agf_z.at[m], to)
+                fed = rc(src, land, agf_s.at[m, 2 * i + cc], agf_f.at[m], to)
+                if i:
+                    passed = at_end & (span == nz - 2)
+                    pl.when(passed)(fed.start)
+                    pl.when(jnp.logical_not(passed) & (span < nz - 1))(far.start)
+                else:
+                    pl.when(c != cc)(far.start)
+                    pl.when(c == cc)(pltpu.make_async_copy(src, land, agf_z.at[m]).start)
+
+    def agf1(m):
+        block = w_f.at[m, relay, x]
+        wait(block, agf_f.at[m])
+        far = rc(block, block, agf_s.at[m, 2 * nz + 1], agf_f.at[m], dev(nz - 1 - relay, x, c, y))
+        pl.when(jnp.logical_not(at_end))(far.start)
+        wait(w_f.at[m, pl.ds(0, nz - 1), x], agf_z.at[m])
+        rc(w_f.at[m, :, x], w_f.at[m, :, x], agf_s.at[m, 2 * nz], agf_x.at[m], xnbr).start()
+
+    def agf2(m):
+        wait(w_f.at[m, :, xb], agf_x.at[m])
+
+    def agf_done(m):
+        for i in range(nz):
+            span = jnp.abs(lax.rem(z + i, nz) - z)
+            for cc in range(2):
+                sent = (span < nz - 1) if i else (c != cc)
+
+                @pl.when(sent)
+                def _():
+                    wait(src_unit(m, cc), agf_s.at[m, 2 * i + cc])
+
+        @pl.when(jnp.logical_not(at_end))
+        def _():
+            wait(w_f.at[m, 0, x], agf_s.at[m, 2 * nz + 1])
+
+        wait(w_f.at[m, :, x], agf_s.at[m, 2 * nz])
+
+    def rsf0(m):
+        rc(w_f.at[m, :, xb], rx_f.at[m], rsf_s.at[m, 2 * nz], rsf_x.at[m], xnbr).start()
+
+    def rsf1(m):
+        wait(rx_f.at[m], rsf_x.at[m])
+        for v in range(2):
+
+            @pl.when(x == v)
+            def _():
+                rx_f[m] = (w_f[m, :, v].astype(F32) + rx_f[m].astype(F32)).astype(BF)
+
+        for i in range(nz):
+            zt = lax.rem(z + i, nz)
+            for cc in range(2):
+                src, land = rx_f.at[m, zt, cc], rz_f.at[m, z, c]
+                far = rc(src, land, rsf_s.at[m, 2 * i + cc], rsf_z.at[m], dev(zt, x, cc, y))
+                if i:
+                    far.start()
+                else:
+                    pl.when(c != cc)(far.start)
+                    pl.when(c == cc)(pltpu.make_async_copy(src, land, rsf_z.at[m]).start)
+
+    def rsf3(m):
+        wait(rz_f.at[m], rsf_z.at[m])
+        halves = []
+        for cc in range(2):
+            total = rz_f[m, 0, cc].astype(F32)
+            for i in range(1, nz):
+                total = total + rz_f[m, i, cc].astype(F32)
+            halves.append(total)
+        return jnp.concatenate(halves, axis=1)
+
+    def rsf_done(m):
+        for i in range(nz):
+            for cc in range(2):
+                if i:
+                    wait(rz_f.at[m, 0, 0], rsf_s.at[m, 2 * i + cc])
+                else:
+
+                    @pl.when(c != cc)
+                    def _():
+                        wait(rz_f.at[m, 0, 0], rsf_s.at[m, cc])
+
+        wait(rx_f.at[m], rsf_s.at[m, 2 * nz])
 
     lo_z = pl.ds(0, kd)
     hi_z = pl.ds(kd, nz - kd)
 
     def at_unit(ref, k, *spot):
-        spot = spot if isinstance(k, str) else (k,) + spot
-        return ref[spot if spot else ...].astype(F32)
+        return ref[(k,) + spot].astype(F32)
 
     def put_unit(ref, k, total, *spot):
-        spot = spot if isinstance(k, str) else (k,) + spot
-        ref[spot if spot else ...] = total.astype(BF)
-
-    def rs_refs(k):
-        if isinstance(k, str):
-            return (w_a, rx_a, ry_a, ry2_a) if k == "a" else (w_o, rx_o, ry_o, ry2_o)
-        return w_f, rx_f, ry_f, ry2_f
+        ref[(k,) + spot] = total.astype(BF)
 
     every = slice(None)
 
@@ -608,7 +692,7 @@
 
     def rs1(k):
         g, rx, ry, ry2, rz, n = rs_unit(k)
-        g_all, rx_all, ry_all, ry2_all = rs_refs(k)
+        g_all, rx_all, ry_all, ry2_all = w_a, rx_a, ry_a, ry2_a
 
         @pl.when(away)
         def _():
@@ -633,7 +717,7 @@
 
     def rs2(k):
         g, rx, ry, ry2, rz, n = rs_unit(k)
-        g_all, rx_all, ry_all, ry2_all = rs_refs(k)
+        g_all, rx_all, ry_all, ry2_all = w_a, rx_a, ry_a, ry2_a
 
         @pl.when(home)
         def _():
@@ -682,10 +766,12 @@
         wait(rz, rs_z.at[n])
         total = None
         for i in range(nz):
-            part = (rz[i] if isinstance(k, str) else rz_f[k, i]).astype(F32)
+            part = rz_a[k, i].astype(F32)
             total = part if total is None else total + part
         return total
 
+    fetch = pltpu.make_async_copy(x_ref, ret, lo_r)
+    fetch.start()
     square = (nrow, nrow)
     on_diag = lax.broadcasted_iota(jnp.int32, square, 0) == lax.broadcasted_iota(
         jnp.int32, square, 1
@@ -698,13 +784,14 @@
     gain1 = column(g1)
     gain2 = column(g2)
     for i, w in enumerate((wq, wk, wv)):
-        src_a[:, i * hw : (i + 1) * hw] = (w[...].astype(F32) * gain1).astype(BF)
-    zsend("a")
+        src_a[i] = (w[...].astype(F32) * gain1).astype(BF)
+        zsend(i)
 
     def stage(j, _):
-        xs[j] = x_ref[deal[j]]
-        return 0
-
+        xs[j] = ret[deal[j]]
+        return 0
+
+    fetch.wait()
     lax.fori_loop(0, groups, stage, 0)
 
     def deal_out(i, _):
@@ -725,11 +812,8 @@
 
     lax.fori_loop(0, groups, deal_out, 0)
 
-    for f in range(nf):
-        cols = slice(f * chunk, (f + 1) * chunk)
-        src_f[f, :, 0:chunk] = (wg[:, cols].astype(F32) * gain2).astype(BF)
-        src_f[f, :, chunk : 2 * chunk] = (wu[:, cols].astype(F32) * gain2).astype(BF)
-        src_f[f, :, 2 * chunk : 3 * chunk] = wd[:, cols]
+    src_f[0] = (wg[...].astype(F32) * gain2).astype(BF)
+    src_f[1] = (wu[...].astype(F32) * gain2).astype(BF)
 
     def rope_rows(i, _):
         ca, sa = tab[0, pl.ds(i, 1), :], tab[1, pl.ds(i, 1), :]
@@ -754,6 +838,7 @@
     ev[...] = jnp.where((row == (col >> 6) * HD + low) & (low < HD), 1.0, 0.0).astype(BF)
 
     length = lens[deal[slot]]
+    other_length = lens[deal[other_slot]]
 
     def live_at(i):
         at = (i * 2 + c) * 32 + lax.broadcasted_iota(jnp.int32, (32, 1), 0)
@@ -768,38 +853,49 @@
     def blk(i):
         return pl.ds(i * (ROWS // 64), ROWS // 64)
 
-    ag1("a")
-    zsend("o")
-    zsend(0)
-
-    @pl.when(home)
-    def _():
-        pltpu.make_async_copy(dy_ref, dybuf, dy_r).start()
-
-    @pl.when(away)
-    def _():
-        rc(dy_ref, dybuf, dy_s, dy_r, swap).start()
-
-    ag2("a")
+    for i in range(3):
+        ag1(i)
+    zsend(3)
+    zsendf(0)
+
+    def gather_dy(mine):
+        pltpu.make_async_copy(dy_ref, mine.at[:, y], dy_r.at[0]).start()
+
+    def send_dy(far):
+        rc(dy_ref, far.at[:, y], dy_s.at[0], dy_r.at[1], ynbr).start()
+
+    for i in range(3):
+        ag2(i)
     wait(xbuf, a2a_r)
+    zsendf(1)
 
     def norm_one(i, _):
         rows_now = xbuf[i].astype(F32)
         r = lax.rsqrt(mean(rows_now * rows_now) + EPS)
-        r1b[i] = jnp.broadcast_to(r, (32, 128))
+        rb[i] = jnp.broadcast_to(r, (32, 128))
         abuf[i, c] = (rows_now * r).astype(BF)
         return 0
 
     lax.fori_loop(0, groups, norm_one, 0, unroll=2)
     swap_start(0, abuf.at[:, c], abuf.at[:, c])
-    ag1("o")
-    zsend(1)
-    ag3("a")
     for i in range(3):
+        ag3(i)
         e = eqk if i < 2 else ev
         wp[:, i * pw : (i + 1) * pw] = mm(
-            NN, w_a[:, :, :, :, i * hw : (i + 1) * hw].reshape(dim, hw), e[...]
+            NN, w_a[i].reshape(dim, hw), e[...]
         ).astype(BF)
+    @pl.when(home)
+    def _():
+        gather_dy(dd0)
+        send_dy(dd1)
+
+    @pl.when(away)
+    def _():
+        gather_dy(dd1)
+        send_dy(dd0)
+
+    ag1(3)
+    zsendf(2)
     wait(abuf.at[:, oth], ex_r.at[0])
 
     query_scale = score_scale * LOG2E
@@ -827,9 +923,8 @@
         return 0
 
     lax.fori_loop(0, nrb, project, 0)
-    ag1(0)
-    ag2("o")
-    zsend(2)
+    ag2(3)
+    agf1(0)
 
     lane = lax.broadcasted_iota(jnp.int32, (ROWS, 256), 1)
     diag = lax.broadcasted_iota(jnp.int32, (ROWS, ROWS), 0) <= lax.broadcasted_iota(
@@ -867,24 +962,42 @@
 
         lax.fori_loop(0, pw // 256, group, 0)
 
+    def hand_dy(mine):
+        wait(mine.at[:, y], dy_r.at[0])
+        wait(mine.at[:, yb], dy_r.at[1])
+        rc(mine, mine, ex_s.at[1], ex_r.at[1], partner).start()
+
     def during_zero():
-        ag1(1)
-        zsend(3)
-        ag3("o")
-        wop[...] = mm(NN, w_o[...].reshape(dim, hw), ev[...]).astype(BF)
+        agf1(1)
 
     def during_one():
-        ag2(0)
-        ag1(2)
-        zsend(4)
+        ag3(3)
+        wop[...] = mm(NN, w_a[3].reshape(dim, hw), ev[...]).astype(BF)
 
     def during_two():
-        ag2(1)
-        ag1(3)
-
-    def mask_dy(i, _):
-        dfb[i, c] = jnp.where(live_at(i), dybuf[i], jnp.zeros((32, dim), BF))
-        return 0
+        pl.when(home)(lambda: hand_dy(dd0))
+        pl.when(away)(lambda: hand_dy(dd1))
+
+    def settle_dy():
+        pl.when(home)(lambda: wait(dd1, ex_r.at[1]))
+        pl.when(away)(lambda: wait(dd0, ex_r.at[1]))
+        wait(dd0, ex_s.at[1])
+
+        def save_dy(i, _):
+            dybuf[i] = dd0[i, c]
+            return 0
+
+        lax.fori_loop(0, groups, save_dy, 0)
+
+        def mask_dy(i, _):
+            at = i * ROWS + lax.broadcasted_iota(jnp.int32, (ROWS, 1), 0)
+            zeros = jnp.zeros((ROWS, dim), BF)
+            for ref, count in ((dd0, length), (dd1, other_length)):
+                masked = jnp.where(at < count, ref[blk(i)].reshape(ROWS, dim), zeros)
+                ref[blk(i)] = masked.reshape(ROWS // 64, 2, 32, dim)
+            return 0
+
+        lax.fori_loop(0, nrb, mask_dy, 0)
 
     def with_steps(part, steps):
         for i in range(nrb):
@@ -894,9 +1007,7 @@
                     step()
 
     with_steps(attend, ((0, during_zero), (1, during_one), (2, during_two)))
-    wait(dybuf, dy_r)
-    lax.fori_loop(0, groups, mask_dy, 0, unroll=2)
-    swap_start(1, dfb.at[:, c], dfb.at[:, c])
+    agf1(2)
 
     def turn(i, _):
         at = pl.ds(pl.multiple_of(i * ROWS, ROWS), ROWS)
@@ -922,103 +1033,171 @@
     lax.fori_loop(0, groups // half_rows, att_other, 0)
     swap_start(2, sb1, rb1)
     lax.fori_loop(0, groups // half_rows, att_own, 0)
-    ag1(4)
     wait(rb1, ex_r.at[2])
+
+    low_lanes = lax.broadcasted_iota(jnp.int32, (32, 128), 1) < 64
 
     def norm_two(i, _):
         att = own[i] + rb1[i].astype(F32)
         x1 = xbuf[i].astype(F32) + jnp.where(live_at(i), att, 0.0)
         x1b[i] = x1
         r = lax.rsqrt(mean(x1 * x1) + EPS)
-        r2b[i] = jnp.broadcast_to(r, (32, 128))
-        bbuf[i, c] = (x1 * r).astype(BF)
-        return 0
-
-    lax.fori_loop(0, groups, norm_two, 0, unroll=2)
-    swap_start(3, bbuf.at[:, c], bbuf.at[:, c])
-    wait(dfb.at[:, oth], ex_r.at[1])
-    wait(bbuf.at[:, oth], ex_r.at[3])
-
-    def ffn(f, _):
-        ag3(f)
-
-        def one(i, _):
-            b = bbuf[blk(i)].reshape(ROWS, dim)
-            d = dfb[blk(i)].reshape(ROWS, dim)
-            w_gu = w_f[f, :, :, :, :, 0 : 2 * chunk].reshape(dim, 2 * chunk)
-            w_d = w_f[f, :, :, :, :, 2 * chunk : 3 * chunk].reshape(dim, chunk)
-            gu = mm(NN, b, w_gu)
-            dh = mm(NN, d, w_d)
-            gate, up = gu[:, 0:chunk], gu[:, chunk:]
-            sg = jax.nn.sigmoid(gate)
-            silu = gate * sg
-            hid = (silu * up).astype(BF)
-            dgate = (dh * up * sg * (1.0 + gate * (1.0 - sg))).astype(BF)
-            dup = (dh * silu).astype(BF)
-            at = pl.ds(pl.multiple_of(i * ROWS, ROWS), ROWS)
-            act[at, 0:chunk] = dgate
-            act[at, chunk : 2 * chunk] = dup
-            act[at, 2 * chunk : 3 * chunk] = hid
-            fpart = mm(NT, hid, w_d).reshape(ROWS // 64, 2, 32, dim)
-            dgu = jnp.concatenate([dgate, dup], axis=1)
-            upart = mm(NT, dgu, w_gu).reshape(ROWS // 64, 2, 32, dim)
-
-            @pl.when(f == 0)
+        rb[i] = jnp.where(low_lanes, rb[i], r)
+        bb0[i, c] = (x1 * r).astype(BF)
+        return 0
+
+    hg = groups // 2
+
+    for hf in range(2):
+        lax.fori_loop(hf * hg, (hf + 1) * hg, norm_two, 0, unroll=2)
+        at = pl.ds(hf * hg, hg)
+        rc(bb0.at[at, c], bb1.at[at, c], b_s.at[1, hf], b_r.at[1, hf], ynbr).start()
+        rc(bb0.at[at, c], bb0.at[at, c], b_s.at[0, hf], b_r.at[0, hf], partner).start()
+
+    def hand_b(hf):
+        at = pl.ds(hf * hg, hg)
+        wait(bb1.at[at, c], b_r.at[1, hf])
+        rc(bb1.at[at, c], bb1.at[at, c], b_s.at[2, hf], b_r.at[2, hf], partner).start()
+
+    def ffn(own_seq, i):
+        b_ref, d_ref, count = (bb0, dd0, length) if own_seq else (bb1, dd1, other_length)
+        base = 0 if own_seq else seq_len
+        b = b_ref[blk(i)].reshape(ROWS, dim)
+        d = d_ref[blk(i)].reshape(ROWS, dim)
+        w_g, w_u, w_d = (w_f[m].reshape(dim, fq) for m in range(3))
+        gate = mm(NN, b, w_g)
+        up = mm(NN, b, w_u)
+        dh = mm(NN, d, w_d)
+        sg = jax.nn.sigmoid(gate)
+        silu = gate * sg
+        hid = (silu * up).astype(BF)
+        dgate = (dh * up * sg * (1.0 + gate * (1.0 - sg))).astype(BF)
+        dup = (dh * silu).astype(BF)
+        at = pl.ds(pl.multiple_of(base + i * ROWS, ROWS), ROWS)
+        act[at, 0:fq] = dgate
+        act[at, fq : 2 * fq] = dup
+        act[at, 2 * fq : 3 * fq] = hid
+        u = (mm(NT, dgate, w_g) + mm(NT, dup, w_u)).reshape(ROWS // 64, 2, 32, dim)
+        n = i if own_seq else i + nrb
+        uacc[blk(i), 0 if own_seq else 1] = jnp.where(c == 0, u[:, 0], u[:, 1])
+
+        @pl.when(n >= 2)
+        def _():
+            wait(usend.at[0], us_s.at[n - 2])
+
+        ring = n % 2
+        usend[ring] = jnp.where(c == 0, u[:, 1], u[:, 0]).astype(BF)
+        part = pl.ds(n * (ROWS // 64), ROWS // 64)
+        rc(usend.at[ring], urecv.at[part], us_s.at[n], us_r.at[n], partner).start()
+        alive = i * ROWS + lax.broadcasted_iota(jnp.int32, (ROWS, 1), 0) < count
+        out = jnp.where(alive, mm(NT, hid, w_d), 0.0).reshape(ROWS // 64, 2, 32, dim)
+
+        @pl.when(home if own_seq else away)
+        def _():
+            facc[blk(i)] = out
+
+        @pl.when(away if own_seq else home)
+        def _():
+            @pl.when(i >= 2)
             def _():
-                facc[blk(i)] = fpart
-                uacc[blk(i)] = upart
-
-            @pl.when(f > 0)
+                wait(fsend.at[0], fs_s.at[i - 2])
+
+            slot_now = i % 2
+            if own_seq:
+                x1 = x1b[blk(i)]
+                fsend[slot_now, :, 0] = (out[:, 0] + jnp.where(c == 0, x1, 0.0)).astype(BF)
+                fsend[slot_now, :, 1] = (out[:, 1] + jnp.where(c == 1, x1, 0.0)).astype(BF)
+            else:
+                fsend[slot_now] = out.astype(BF)
+            rc(fsend.at[slot_now], frecv.at[blk(i)], fs_s.at[i], fs_r.at[i], partner).start()
+
+    settle_dy()
+    for m in range(3):
+        agf2(m)
+    for hf in range(2):
+        wait(bb0.at[pl.ds(hf * hg, hg), oth], b_r.at[0, hf])
+
+    def ffn_own(i, _):
+        ffn(True, i)
+
+        @pl.when(i == nrb - 2)
+        def _():
+            hand_b(0)
+
+        return 0
+
+    lax.fori_loop(0, nrb, ffn_own, 0)
+    hand_b(1)
+
+    per = ROWS // 64
+
+    def join_u(i):
+        at = pl.ds((nrb + i) * per, per)
+        wait(urecv.at[at], us_r.at[nrb + i])
+        sb1[pl.ds(i * per, per)] = (uacc[blk(i), 1] + urecv[at].astype(F32)).astype(BF)
+        at = pl.ds(i * per, per)
+        rc(sb1.at[at], rb1.at[at], uy_s.at[0, i], uy_r.at[0, i], ynbr).start()
+
+    def ffn_other(i, _):
+        for hf in range(2):
+
+            @pl.when(i == hf * nrb // 2)
             def _():
-                facc[blk(i)] += fpart
-                uacc[blk(i)] += upart
-
+                wait(bb1.at[pl.ds(hf * hg, hg), oth], b_r.at[2, hf])
+
+        ffn(False, i)
+
+        @pl.when(i >= 1)
+        def _():
+            join_u(i - 1)
+
+        return 0
+
+    wait(sb1, ex_s.at[2])
+    lax.fori_loop(0, nrb, ffn_other, 0)
+    join_u(nrb - 1)
+
+    for i in range(nrb):
+        wait(frecv.at[blk(i)], fs_r.at[i])
+
+    def join_out(i, _):
+        sb2[i] = (facc[i, yb] + frecv[i, yb].astype(F32)).astype(BF)
+        mine = facc[i, y] + frecv[i, y].astype(F32)
+        own[i] = mine + jnp.where(home, x1b[i], 0.0)
+        return 0
+
+    lax.fori_loop(0, groups, join_out, 0)
+    rc(sb2, rb2, uy_s.at[1, 0], uy_r.at[1, 0], ynbr).start()
+
+    def weight_grad(m, refs, first):
+        agf_done(m)
+        rows_half = half // 64
+
+        def one_half(part, _):
+            feats = pl.ds(pl.multiple_of(part * half, 128), half)
+            t = None
+            for n, ref in enumerate(refs):
+                left = ref[:, :, :, feats].reshape(seq_len, half)
+                term = mm(TN, left, act[n * seq_len : (n + 1) * seq_len, first : first + fq])
+                t = term if t is None else t + term
+            facc[pl.ds(part * rows_half, rows_half), :, :, 0:fq] = t.reshape(rows_half, 2, 32, fq)
             return 0
 
-        lax.fori_loop(0, nrb, one, 0)
-        ag_done(f)
-        for m in range(2):
-            feats = slice(m * half, (m + 1) * half)
-            zs = slice(m * nz // 2, (m + 1) * nz // 2)
-            left = bbuf[:, :, :, feats].reshape(seq_len, half)
-            t = mm(TN, left, act[:, 0 : 2 * chunk]).astype(BF)
-            w_f[f, zs, :, :, :, 0 : 2 * chunk] = t.reshape(nz // 2, 2, 2, nrow, 2 * chunk)
-            left = dfb[:, :, :, feats].reshape(seq_len, half)
-            t = mm(TN, left, act[:, 2 * chunk : 3 * chunk]).astype(BF)
-            w_f[f, zs, :, :, :, 2 * chunk : 3 * chunk] = t.reshape(nz // 2, 2, 2, nrow, chunk)
-        rs0(f)
-
-        @pl.when(f + 2 < nf)
-        def _():
-            ag2(f + 2)
-
-        @pl.when(f >= 1)
-        def _():
-            rs1(f - 1)
-
-        @pl.when(f >= 2)
-        def _():
-            rs2(f - 2)
-
-        return 0
-
-    lax.fori_loop(0, nf, ffn, 0)
-
-    wait(sb1, ex_s.at[2])
-
-    def cast_u(i, _):
-        sb1[i] = uacc[i, oth].astype(BF)
-        return 0
-
-    def cast_f(i, _):
-        sb2[i] = facc[i, oth].astype(BF)
-        return 0
-
-    lax.fori_loop(0, groups, cast_u, 0)
-    swap_start(4, sb1, rb1)
-    lax.fori_loop(0, groups, cast_f, 0)
-    swap_start(5, sb2, rb2)
-    rs1(nf - 1)
+        lax.fori_loop(0, 2, one_half, 0)
+        for part in range(2):
+            zs = slice(part * nz // 2, (part + 1) * nz // 2)
+            t = facc[part * rows_half : (part + 1) * rows_half, :, :, 0:fq].reshape(half, fq)
+            w_f[m, zs] = t.astype(BF).reshape(nz // 2, 2, 2, nrow, fq)
+        rsf0(m)
+
+    weight_grad(0, (bb0, bb1), 0)
+    weight_grad(1, (bb0, bb1), fq)
+    pl.semaphore_signal(free, inc=1, device_id=partner, device_id_type=MESH)
+    weight_grad(2, (dd0, dd1), 2 * fq)
+    rsf1(0)
+    for i in range(nrb):
+        at = pl.ds(i * per, per)
+        wait(urecv.at[at], us_r.at[i])
 
     @pl.when(home)
     def _():
@@ -1028,35 +1207,27 @@
     def _():
         wait(xs, a2a_s)
 
-    wait(rb1, ex_r.at[4])
-    wait(rb2, ex_r.at[5])
-    wait(bbuf.at[:, c], ex_s.at[3])
+    for hf in range(2):
+        at = pl.ds(hf * hg, hg)
+        wait(bb0.at[at, c], b_s.at[0, hf])
+        wait(bb0.at[at, c], b_s.at[1, hf])
+    for i in range(nrb):
+        wait(rb1.at[pl.ds(i * per, per)], uy_r.at[0, i])
 
     def norm_three(i, _):
         alive = live_at(i)
         x1 = x1b[i]
-        r = r2b[i][:, 0:1]
+        r = rb[i][:, 64:65]
         n = x1 * r
-        u = uacc[i, c] + rb1[i].astype(F32)
+        u = uacc[i, 0] + urecv[i].astype(F32) + rb1[i].astype(F32)
         dx1 = dybuf[i].astype(F32) + r * (u - n * mean(u * n))
-        bbuf[i, c] = jnp.where(alive, dx1, 0.0).astype(BF)
-        ffn_out = facc[i, c] + rb2[i].astype(F32)
-        xs[i] = (x1 + jnp.where(alive, ffn_out, 0.0)).astype(BF)
+        bb0[i, c] = jnp.where(alive, dx1, 0.0).astype(BF)
         x1b[i] = dx1
         return 0
 
     lax.fori_loop(0, groups, norm_three, 0, unroll=2)
-    swap_start(6, bbuf.at[:, c], bbuf.at[:, c])
-
-    @pl.when(home)
-    def _():
-        pltpu.make_async_copy(xs, lo_ref, lo_r).start()
-
-    @pl.when(away)
-    def _():
-        rc(xs, lo_ref, lo_s, lo_r, swap).start()
-
-    rs2(nf - 2)
+    pl.semaphore_wait(free, 1)
+    swap_start(6, bb0.at[:, c], bb0.at[:, c])
 
     def turn_k(i, _):
         at = pl.ds(pl.multiple_of(i * ROWS, ROWS), ROWS)
@@ -1072,24 +1243,27 @@
     pick = jnp.where(
         (lax.broadcasted_iota(jnp.int32, (16, pw), 1) >> 6) == heads16, 1.0, 0.0
     ).astype(BF)
-    wait(bbuf.at[:, oth], ex_r.at[6])
+    wait(bb0.at[:, oth], ex_r.at[6])
+
+    for hf in range(2):
+        wait(bb1.at[pl.ds(hf * hg, hg), c], b_s.at[2, hf])
 
     def out_back(i, _):
         at = pl.ds(pl.multiple_of(i * ROWS, ROWS), ROWS)
-        t = mm(NN, bbuf[blk(i)].reshape(ROWS, dim), wop[...]).astype(BF)
-        dob[blk(i)] = t.reshape(ROWS // 64, 2, 32, pw)
+        t = mm(NN, bb0[blk(i)].reshape(ROWS, dim), wop[...]).astype(BF)
+        bb1[blk(i), :, :, 0:pw] = t.reshape(ROWS // 64, 2, 32, pw)
         prod = t.astype(F32) * ob[blk(i)].reshape(ROWS, pw).astype(F32)
         delta[:, at] = mm(NT, pick, prod.astype(BF))
         return 0
 
     lax.fori_loop(0, nrb, out_back, 0)
-    ag_done("o")
+    ag_done(3)
     for m in range(2):
-        left = bbuf[:, :, :, m * half : (m + 1) * half].reshape(seq_len, half)
+        left = bb0[:, :, :, m * half : (m + 1) * half].reshape(seq_len, half)
         t = mm(TN, left, ob[...].reshape(seq_len, pw)).astype(BF)
         zs = slice(m * nz // 2, (m + 1) * nz // 2)
-        w_o[zs] = mm(NT, t, ev[...]).astype(BF).reshape(nz // 2, 2, 2, nrow, hw)
-    rs0("o")
+        w_a[3, zs] = mm(NT, t, ev[...]).astype(BF).reshape(nz // 2, 2, 2, nrow, hw)
+    rs0(3)
 
     def attend_back(i):
         keys = (i + 1) * ROWS
@@ -1097,7 +1271,7 @@
         def group(g, _):
             lanes = pl.ds(pl.multiple_of(g * 256, 256), 256)
             q = rows_of(qb, i * ROWS, ROWS, lanes)
-            d = rows_of(dob, i * ROWS, ROWS, lanes)
+            d = rows_of(bb1, i * ROWS, ROWS, lanes)
             for hh in range(4):
                 qm = jnp.where(((lane >> 5) & 3) == hh, q, jnp.zeros_like(q))
                 dm = jnp.where((lane >> 6) == hh, d, jnp.zeros_like(d))
@@ -1136,9 +1310,18 @@
 
         lax.fori_loop(0, pw // 256, group, 0)
 
+    def back_zero():
+        rsf1(1)
+
+    def back_one():
+        rsf1(2)
+
+    def back_two():
+        rs1(3)
+
     with_steps(
         attend_back,
-        ((0, lambda: rs2(nf - 1)), (1, lambda: rs1("o")), (2, lambda: rs2("o"))),
+        ((0, back_zero), (1, back_one), (2, back_two)),
     )
 
     def turn_back(i, _):
@@ -1158,17 +1341,27 @@
         return 0
 
     lax.fori_loop(0, nrb, turn_back, 0)
-    ag_done("a")
     for t, (src, e) in enumerate(((qb, eqk), (kb, eqk), (vb, ev))):
+        ag_done(t)
         for m in range(2):
             left = abuf[:, :, :, m * half : (m + 1) * half].reshape(seq_len, half)
             part = mm(TN, left, src[...].reshape(seq_len, pw)).astype(BF)
             zs = slice(m * nz // 2, (m + 1) * nz // 2)
-            w_a[zs, :, :, :, t * hw : (t + 1) * hw] = (
-                mm(NT, part, e[...]).astype(BF).reshape(nz // 2, 2, 2, nrow, hw)
-            )
-    rs0("a")
-    wait(sb1, ex_s.at[4])
+            w_a[t, zs] = mm(NT, part, e[...]).astype(BF).reshape(nz // 2, 2, 2, nrow, hw)
+        rs0(t)
+    for hf in range(2):
+        for i in range(hf * nrb // 2, (hf + 1) * nrb // 2):
+            wait(sb1.at[pl.ds(i * per, per)], uy_s.at[0, i])
+
+    wait(rb2, uy_r.at[1, 0])
+
+    def finish_out(i, _):
+        sb2[i] = (own[i] + rb2[i].astype(F32)).astype(BF)
+        return 0
+
+    wait(sb2, uy_s.at[1, 0])
+    lax.fori_loop(0, groups, finish_out, 0)
+    pltpu.make_async_copy(sb2, lo_ref, lo_r).start()
 
     def da_rows(at, which):
         total = None
@@ -1190,17 +1383,13 @@
     lax.fori_loop(0, groups // half_rows, da_other, 0)
     swap_start(7, sb1, rb1)
     lax.fori_loop(0, groups // half_rows, da_own, 0)
-
-    @pl.when(away)
-    def _():
-        wait(xs, lo_s)
-
-    wait(lo_ref, lo_r)
+    rs2(3)
+
     wait(rb1, ex_r.at[7])
 
     def norm_four(i, _):
         rows_now = xbuf[i].astype(F32)
-        r = r1b[i][:, 0:1]
+        r = rb[i][:, 0:1]
         n = rows_now * r
         u = own[i] + rb1[i].astype(F32)
         dx = x1b[i] + r * (u - n * mean(u * n))
@@ -1218,26 +1407,21 @@
         return 0
 
     lax.fori_loop(0, groups, norm_four, 0)
-    rs1("a")
-
-    def finish_f(f, total):
-        sums = jnp.zeros((nrow, 1), F32) if total is None else total
-        t = rs3(f)
-        at = pl.ds(pl.multiple_of(f * chunk, chunk), chunk)
-        dg, du = t[:, 0:chunk], t[:, chunk : 2 * chunk]
-        dg_out[:, at] = dg * gain2
-        du_out[:, at] = du * gain2
-        dd_out[:, at] = t[:, 2 * chunk : 3 * chunk]
-        both = dg * wg[:, at].astype(F32) + du * wu[:, at].astype(F32)
-        return sums + jnp.sum(both, axis=1, keepdims=True)
-
-    sums2 = lax.fori_loop(0, nf, finish_f, jnp.zeros((nrow, 1), F32))
-    rs2("a")
-    do_out[...] = rs3("o")
-    t = rs3("a")
+    for i in range(3):
+        rs1(i)
+    for i in range(3):
+        rs2(i)
+
+    d_g, d_u = rsf3(0), rsf3(1)
+    dg_out[...] = d_g * gain2
+    du_out[...] = d_u * gain2
+    both = d_g * wg[...].astype(F32) + d_u * wu[...].astype(F32)
+    sums2 = jnp.sum(both, axis=1, keepdims=True)
+    dd_out[...] = rsf3(2)
+    do_out[...] = rs3(3)
     sums1 = jnp.zeros((nrow, 1), F32)
     for i, (w, out) in enumerate(((wq, dq_out), (wk, dk_out), (wv, dv_out))):
-        part = t[:, i * hw : (i + 1) * hw]
+        part = rs3(i)
         out[...] = part * gain1
         sums1 = sums1 + jnp.sum(part * w[...].astype(F32), axis=1, keepdims=True)
     first_half = lax.broadcasted_iota(jnp.int32, (nrow, 128), 1) < 64
@@ -1250,25 +1434,26 @@
         def find(j, at):
             return jnp.where(deal[j] == s, j, at)
 
-        gi_ref[s] = ret[lax.fori_loop(0, groups, find, 0)]
-        return 0
-
+        sb2[s] = ret[lax.fori_loop(0, groups, find, 0)]
+        return 0
+
+    wait(sb2, lo_r)
     lax.fori_loop(0, groups, restore, 0)
+    give = pltpu.make_async_copy(sb2, gi_ref, lo_r)
+    give.start()
     wait(gr, gg_r)
     both = gs[...] + gr[...]
     dg1_out[...] = jnp.sum(jnp.where(on_diag, both[:, 0:1], 0.0), axis=0, keepdims=True)
     dg2_out[...] = jnp.sum(jnp.where(on_diag, both[:, 64:65], 0.0), axis=0, keepdims=True)
 
     wait(gs, gg_s)
-    for f in range(nf):
-        rs_done(f)
-    rs_done("o")
-    rs_done("a")
-
-    @pl.when(away)
-    def _():
-        wait(dybuf, dy_s)
-
+    for m in range(3):
+        rsf_done(m)
+    for i in range(4):
+        rs_done(i)
+
+    wait(dybuf, dy_s.at[0])
+    give.wait()
     @pl.when(home)
     def _():
         wait(xs.at[pl.ds(0, groups - 1)], ret_s)
@@ -1278,9 +1463,10 @@
         wait(xs, ret_s)
 
     wait(abuf.at[:, c], ex_s.at[0])
-    wait(dfb.at[:, c], ex_s.at[1])
-    wait(sb2, ex_s.at[5])
-    wait(bbuf.at[:, c], ex_s.at[6])
+    for i in range(2):
+        wait(usend.at[i], us_s.at[2 * nrb - 2 + i])
+        wait(fsend.at[i], fs_s.at[nrb - 2 + i])
+    wait(bb0.at[:, c], ex_s.at[6])
     wait(sb1, ex_s.at[7])
 
 
@@ -1300,8 +1486,7 @@
     groups, piece_rows, dim = x_given.shape
     hw = query_weight.shape[1]
     local_hidden = gate_weight.shape[1]
-    chunk = 256
-    nf = local_hidden // chunk
+    fq = local_hidden // 2
     nz = groups // 4
     rows = query_weight.shape[0]
     pw = hw // HD * 64
@@ -1327,12 +1512,12 @@
             pltpu.VMEM(lead + (nz, rows, width), BF),
         ]
 
-    units = nf + 2
+    nrb = seq_len // ROWS
     dma = pltpu.SemaphoreType.DMA
     scratch = (
         [pltpu.VMEM(blocks, BF)] * 3
-        + [pltpu.VMEM((rows, 3 * hw), BF), pltpu.VMEM((nf, rows, 3 * chunk), BF)]
-        + [gathered(3 * hw), gathered(hw), gathered(3 * chunk, (nf,))]
+        + [pltpu.VMEM((3, rows, hw), BF), pltpu.VMEM((2, rows, local_hidden), BF)]
+        + [gathered(hw, (4,)), gathered(fq, (3,))]
         + [pltpu.VMEM((dim, 3 * pw), BF), pltpu.VMEM((dim, pw), BF)]
         + [pltpu.VMEM((hw, pw), BF)] * 2
         + [pltpu.VMEM((seq_len, 128), F32)] * 2
@@ -1345,32 +1530,38 @@
         + [pltpu.VMEM(blocks, F32)]
         + [pltpu.VMEM(blocks, BF)] * 4
         + [pltpu.VMEM(blocks, F32)]
-        + [pltpu.VMEM((groups, piece_rows, 128), F32)] * 2
-        + [pltpu.VMEM(pairs + (dim,), BF)] * 2
+        + [pltpu.VMEM((groups, piece_rows, 128), F32)]
+        + [pltpu.VMEM(pairs + (dim,), BF)] * 4
         + [pltpu.VMEM(pairs + (dim,), F32)] * 2
-        + [pltpu.VMEM((seq_len, 3 * chunk), BF)]
-        + [pltpu.VMEM(pairs + (pw,), BF)]
+        + [pltpu.VMEM((2 * seq_len, 3 * fq), BF)]
         + [pltpu.VMEM((16, seq_len), F32)]
-        + landing(3 * hw)
-        + landing(hw)
-        + landing(3 * chunk, (nf,))
+        + [pltpu.VMEM((2 * groups, piece_rows, dim), BF), pltpu.VMEM(pairs + (dim,), BF)]
+        + [pltpu.VMEM((2, ROWS // 64, piece_rows, dim), BF)]
+        + [pltpu.VMEM((2, ROWS // 64, 2, piece_rows, dim), BF)]
+        + landing(hw, (4,))
+        + [pltpu.VMEM((3, nz, 2, rows, fq), BF)] * 2
         + [pltpu.VMEM(blocks, BF)]
-        + [pltpu.VMEM((rows, 128), F32)] * 3
+        + [pltpu.VMEM((rows, 128), F32)] * 2
+        + [dma(()), dma(()), dma((1,)), dma((2,))]
+        + [dma((4,)), dma((4,)), dma((4,)), dma((4, 2)), dma((4, nz + 3))]
+        + [dma((4, 2)), dma((4, 2)), dma((4,)), dma((4, 2 * nz + 2))]
+        + [dma((3,)), dma((3,)), dma((3,)), dma((3, 2 * nz + 2))]
+        + [dma((3,)), dma((3,)), dma((3, 2 * nz + 1))]
+        + [dma((8,)), dma((8,)), dma((3, 2)), dma((3, 2))]
+        + [dma((2 * nrb,)), dma((2 * nrb,)), dma((nrb,)), dma((nrb,))]
+        + [dma((2, nrb)), dma((2, nrb)), dma(())]
         + [dma(())] * 4
-        + [dma((units,)), dma((units,)), dma((units,)), dma((units, 2)), dma((units, nz + 3))]
-        + [dma((units, 2)), dma((units, 2)), dma((units,)), dma((units, 2 * nz + 2))]
-        + [dma((8,)), dma((8,))]
-        + [dma(())] * 6
+        + [pltpu.SemaphoreType.REGULAR]
     )
     small = jax.ShapeDtypeStruct((rows, hw), F32)
     wide = jax.ShapeDtypeStruct((rows, local_hidden), F32)
     piece = jax.ShapeDtypeStruct(blocks, BF)
     outs = pl.pallas_call(
-        functools.partial(fused_kernel, (nz, nf, dim, hw, chunk, rows)),
+        functools.partial(fused_kernel, (nz, dim, hw, fq, rows)),
         out_shape=[piece, piece, small, small, small, small, wide, wide, wide]
         + [jax.ShapeDtypeStruct((1, rows), F32)] * 2,
-        in_specs=[sm, sm, vm, anym] + [vm] * 10,
-        out_specs=[anym] + [vm] * 10,
+        in_specs=[sm, sm, anym, anym] + [vm] * 10,
+        out_specs=[anym] * 2 + [vm] * 9,
         scratch_shapes=scratch,
         compiler_params=pltpu.CompilerParams(
             collective_id=0, has_side_effects=True, vmem_limit_bytes=VMEM_LIMIT

time: 219 us -> 213 us (0.973)
  Pallas kernels: 218 us -> 212 us
    pallas_call x1, Pallas kernels: 215 us -> 209 us  [fused_body(): pl.pallas_call(functools.partial(fused_kernel, (nz, dim, hw, fq, rows)),...]
where the time goes in v3:
time: 213 us
  Pallas kernels  212 us (100%)
    pallas_call x1, Pallas kernels, fused_body(): pl.pallas_call(functools.partial(fused_kernel, (nz, dim, hw, fq, rows)),...  209 us

profile of v3, /device:TPU:25, one launch (start us, length us, event | category | flops | bytes accessed | tf_op | source)
XLA Modules:
  0.0 212.6 jit_solution(10604382340930889104)
XLA Ops:
  0.6 208.6 %layer.1 = (bf16[16,32,768]{2,1,0:T(8,128)(2,1)}, bf16[16,32,768]{2,1,0:T(8,128)(2,1)}, f32[48,384]{1,0:T(8,128)}, f32[48,384]{1,0:T(8,128)}, f32[48,384]{1,0:T(...) custom-call(s32[16]{0:T(128)} %deal.1, s32[16]{0:T(128)} %lens.1, ...), custom_call_target="tpu_custom_call" | custom-call | tf_op jit(solution)/shard_map/layer/pallas_call | solution.py:1559
  209.3 3.2 %results.1 = (bf16[16,32,768]{2,1,0:T(8,128)(2,1)}, bf16[16,32,768]{2,1,0:T(8,128)(2,1)}, f32[48,384]{1,0:T(8,128)}, f32[48,384]{1,0:T(8,128)}, f32[48,384]{1,0:...) custom-call(bf16[16,32,768]{2,1,0:T(8,128)(2,1)} %get-tuple-element., ...), custom_call_target="tpu_custom_call" | custom-call | tf_op jit(solution)/shard_map/results/pallas_call | solution.py:1576

commit v4 on v3

--- a/solution.py
+++ b/solution.py
@@ -1194,7 +1194,6 @@
     weight_grad(1, (bb0, bb1), fq)
     pl.semaphore_signal(free, inc=1, device_id=partner, device_id_type=MESH)
     weight_grad(2, (dd0, dd1), 2 * fq)
-    rsf1(0)
     for i in range(nrb):
         at = pl.ds(i * per, per)
         wait(urecv.at[at], us_r.at[i])
@@ -1228,6 +1227,7 @@
     lax.fori_loop(0, groups, norm_three, 0, unroll=2)
     pl.semaphore_wait(free, 1)
     swap_start(6, bb0.at[:, c], bb0.at[:, c])
+    rsf1(0)
 
     def turn_k(i, _):
         at = pl.ds(pl.multiple_of(i * ROWS, ROWS), ROWS)
@@ -1311,13 +1311,13 @@
         lax.fori_loop(0, pw // 256, group, 0)
 
     def back_zero():
+        pass
+
+    def back_one():
         rsf1(1)
 
-    def back_one():
+    def back_two():
         rsf1(2)
-
-    def back_two():
-        rs1(3)
 
     with_steps(
         attend_back,
@@ -1383,7 +1383,7 @@
     lax.fori_loop(0, groups // half_rows, da_other, 0)
     swap_start(7, sb1, rb1)
     lax.fori_loop(0, groups // half_rows, da_own, 0)
-    rs2(3)
+    rs1(3)
 
     wait(rb1, ex_r.at[7])
 
@@ -1409,6 +1409,7 @@
     lax.fori_loop(0, groups, norm_four, 0)
     for i in range(3):
         rs1(i)
+    rs2(3)
     for i in range(3):
         rs2(i)
 

time: 213 us -> 209 us (0.981)
  Pallas kernels: 212 us -> 208 us
    pallas_call x1, Pallas kernels: 209 us -> 205 us  [fused_body(): pl.pallas_call(functools.partial(fused_kernel, (nz, dim, hw, fq, rows)),...]
where the time goes in v4:
time: 209 us
  Pallas kernels  208 us (100%)
    pallas_call x1, Pallas kernels, fused_body(): pl.pallas_call(functools.partial(fused_kernel, (nz, dim, hw, fq, rows)),...  205 us

profile of v4, /device:TPU:25, one launch (start us, length us, event | category | flops | bytes accessed | tf_op | source)
XLA Modules:
  0.0 209.2 jit_solution(3244093178681446752)
XLA Ops:
  0.6 205.2 %layer.1 = (bf16[16,32,768]{2,1,0:T(8,128)(2,1)}, bf16[16,32,768]{2,1,0:T(8,128)(2,1)}, f32[48,384]{1,0:T(8,128)}, f32[48,384]{1,0:T(8,128)}, f32[48,384]{1,0:T(...) custom-call(s32[16]{0:T(128)} %deal.1, s32[16]{0:T(128)} %lens.1, ...), custom_call_target="tpu_custom_call" | custom-call | tf_op jit(solution)/shard_map/layer/pallas_call | solution.py:1560
  205.9 3.2 %results.1 = (bf16[16,32,768]{2,1,0:T(8,128)(2,1)}, bf16[16,32,768]{2,1,0:T(8,128)(2,1)}, f32[48,384]{1,0:T(8,128)}, f32[48,384]{1,0:T(8,128)}, f32[48,384]{1,0:...) custom-call(bf16[16,32,768]{2,1,0:T(8,128)(2,1)} %get-tuple-element., ...), custom_call_target="tpu_custom_call" | custom-call | tf_op jit(solution)/shard_map/results/pallas_call | solution.py:1577
